TPU v7x, 32 devices: a whole 2x2x4 slice. The times are simulated.
32 devices in a mesh: member: 2 (over y), lat: 4 (over z), lev: 2 (over x), fld: 2 (over core).
Axes of the slice: x: 2, y: 2, z: 4, core: 2. Of those that a mesh axis runs over, the one named last changes fastest.
Arguments:
- tracer: bfloat16 [8, 800, 1600], P('member', 'lat', ('lev', 'fld')), parts along dimension 0, may hold values from -6 to 6
- wind_east: bfloat16 [8, 800, 1600], P('member', 'lat', ('lev', 'fld')), parts along dimension 0, may hold values from -3 to 3
- wind_north: bfloat16 [8, 800, 1600], P('member', 'lat', ('lev', 'fld')), parts along dimension 0, may hold values from -3 to 3
- keep_m: int32 [800], P('lat'), may hold values from 9 to 400, as said below
- slot_wave: int32 [400], replicated, may hold values from 0 to 399, each once
Outputs:
- spectral: float32 [8, 400, 2, 400], P(('member', 'lev', 'fld'), 'lat'), parts along dimension 0
There are 2 independent parts, one for each index of `member`. A program takes and returns all parts, laid end to end along the dimension named above; an argument that names none is the same for every part. Nothing has to cross between parts.
Inputs may be any that keep to these rules, and one draw needn't show every extreme that they name: keep_m equals 400 at rows 399 and 400, and 9 at rows 0 and 799. Slot s of the output holds wavenumber slot_wave[s]; values of 400 or more mark empty slots.
All inputs are finite; a program needn't handle non-finite values.
Results may differ from a plain program's by a relative error of at most 0.0003.
Values may be sent and summed in bfloat16 or wider, within the bound.
A program may use at most 64 MiB of HBM per device.

v0:
```python
import math

import jax
import jax.numpy as jnp
from jax import lax
from jax.sharding import PartitionSpec as P

M = 400
NLAT = 800
NLON = 1600


precise = lax.Precision.HIGHEST
block_rows = 16


def with_halo(block, sides, width):
    for axis, dim in sides:
        count = lax.axis_size(axis)
        forward = [(i, i + 1) for i in range(count - 1)]
        forward.append((count - 1, 0))
        backward = [(target, source) for source, target in forward]
        low = lax.ppermute(
            lax.slice_in_dim(block, block.shape[dim] - width, None, axis=dim), axis, forward
        )
        high = lax.ppermute(lax.slice_in_dim(block, 0, width, axis=dim), axis, backward)
        block = jnp.concatenate([low, block, high], axis=dim)
    return block


def fourier_table(wave_ids, lon_count):
    grid_index = jnp.arange(lon_count, dtype=jnp.int32)
    phase_index = wave_ids[:, None] * grid_index[None, :] % lon_count
    angles = 2.0 * math.pi / lon_count * phase_index.astype(jnp.float32)
    factor = 1.0 / math.sqrt(lon_count)
    return jnp.stack([jnp.cos(angles), -jnp.sin(angles)], axis=1) * factor


def advect(padded, east_wind, north_wind, first_row, lat_total):
    rows_here = padded.shape[1] - 2
    row_ids = first_row - 1 + jnp.arange(rows_here + 2, dtype=jnp.int32)
    inside = ((row_ids >= 0) & (row_ids < lat_total)).astype(jnp.float32)
    field_rows = padded.astype(jnp.float32) * inside[None, :, None]
    centre = field_rows[:, 1:-1, 1:-1]
    east_diff = field_rows[:, 1:-1, 2:] - field_rows[:, 1:-1, :-2]
    north_diff = field_rows[:, 2:, 1:-1] - field_rows[:, :-2, 1:-1]
    return (
        centre
        - 0.5 * east_wind.astype(jnp.float32) * east_diff
        - 0.5 * north_wind.astype(jnp.float32) * north_diff
    )


def legendre_setup(wave_ids, trunc_count, lat_total, lat_used):
    degree = jnp.minimum(wave_ids, trunc_count - 1).astype(jnp.float32)
    counter = jnp.arange(1, trunc_count, dtype=jnp.float32)
    log_terms = jnp.log1p(0.5 / counter)
    log_norm = jnp.sum(
        jnp.where(counter[None, :] <= degree[:, None], log_terms[None, :], 0.0), axis=1
    )
    colatitude = math.pi / lat_total * (jnp.arange(lat_used, dtype=jnp.float32) + 0.5)
    sine_rows = jnp.sin(colatitude)
    cosines = jnp.cos(colatitude)
    start_log = (
        0.5 * (log_norm[:, None] - math.log(2.0)) + degree[:, None] * jnp.log(sine_rows)[None, :]
    )
    return (degree, cosines, start_log)


def legendre_rows(recurrence, degree, cosines, first_order):
    before, current, log_scale = recurrence
    rows_list = [current]
    for offset in range(1, block_rows + 1):
        order_value = (first_order + offset).astype(jnp.float32)
        total_degree = degree[:, None] + order_value
        growth = jnp.sqrt(
            (4.0 * total_degree * total_degree - 1.0)
            / (total_degree * total_degree - degree[:, None] * degree[:, None])
        )
        lower_degree = total_degree - 1.0
        damping = jnp.sqrt(
            (lower_degree * lower_degree - degree[:, None] * degree[:, None])
            / jnp.maximum(4.0 * lower_degree * lower_degree - 1.0, 1.0)
        )
        advanced = growth * (cosines[None, :] * current - damping * before)
        before, current = (current, advanced)
        if offset < block_rows:
            rows_list.append(current)
    biggest = jnp.maximum(jnp.abs(before), jnp.abs(current))
    table_rows = jnp.stack(rows_list, axis=1) * jnp.exp(log_scale)[:, None, :]
    return (table_rows, (before / biggest, current / biggest, log_scale + jnp.log(biggest)))


def legendre_sweep(legendre_basis, contract, level_count, trunc_count):
    degree, cosines, start_log = legendre_basis
    slot_count = degree.shape[0]
    lat_used = cosines.shape[0]
    before = jnp.zeros((slot_count, lat_used), jnp.float32)
    current = jnp.ones((slot_count, lat_used), jnp.float32)
    result_init = jnp.zeros((level_count, slot_count, 2, trunc_count), jnp.float32)

    def advance(block_index, loop_carry):
        recurrence, result_now = loop_carry
        first_order = block_index * block_rows
        table_rows, recurrence = legendre_rows(recurrence, degree, cosines, first_order)
        orders = (first_order + jnp.arange(block_rows, dtype=jnp.int32)).astype(jnp.float32)
        inside_triangle = (orders[None, :] < trunc_count - degree[:, None]).astype(jnp.float32)
        partial_value = contract(table_rows * inside_triangle[:, :, None])
        result_now = lax.dynamic_update_slice_in_dim(result_now, partial_value, first_order, 3)
        return (recurrence, result_now)

    finished = lax.fori_loop(
        0, trunc_count // block_rows, advance, ((before, current, start_log), result_init)
    )
    return finished[1]


def shards(tracer, wind_east, wind_north, keep_m, slot_wave):
    lat_rows = tracer.shape[1]
    first_row = lax.axis_index("lat") * lat_rows
    fourier_matrix = fourier_table(slot_wave, NLON)
    padded = with_halo(tracer, (("lat", 1), (("lev", "fld"), 2)), 1)
    advected = advect(padded, wind_east, wind_north, first_row, NLAT)
    fourier = jnp.einsum(
        "sck,ijk->scij",
        fourier_matrix,
        lax.all_to_all(advected, ("lev", "fld"), split_axis=0, concat_axis=2, tiled=True),
        precision=precise,
    )
    kept_mask = (slot_wave[:, None] < keep_m[None, :]).astype(jnp.float32)
    fourier = fourier * kept_mask[:, None, None, :]
    spectral_in = lax.all_to_all(fourier, "lat", split_axis=0, concat_axis=3, tiled=True)
    slot_count = spectral_in.shape[0]
    my_waves = lax.dynamic_slice_in_dim(slot_wave, lax.axis_index("lat") * slot_count, slot_count)
    sines_all = jnp.sin(math.pi / NLAT * (jnp.arange(NLAT, dtype=jnp.float32) + 0.5))
    weighted = spectral_in * (sines_all * math.sqrt(2.0 / NLAT))[None, None, None, :]
    legendre_basis = legendre_setup(my_waves, M, NLAT, NLAT)

    def contract(table_rows):
        return jnp.einsum("stj,scij->isct", table_rows, weighted, precision=precise)

    return legendre_sweep(legendre_basis, contract, weighted.shape[2], M)


def solution(mesh):
    return jax.shard_map(
        shards,
        mesh=mesh,
        in_specs=(
            P("member", "lat", ("lev", "fld")),
            P("member", "lat", ("lev", "fld")),
            P("member", "lat", ("lev", "fld")),
            P("lat"),
            P(),
        ),
        out_specs=P(("member", "lev", "fld"), "lat", None, None),
        check_vma=False,
    )
```

profile of v0, /device:TPU:0, one launch (start us, length us, event | category | flops | bytes accessed | tf_op | source)
XLA Modules:
  0.0 815.6 jit_solution(2466917130893633722)
XLA Ops:
  0.8 3.1 collective-permute-start
  3.9 2.1 collective-permute-start.1
  10.7 3.9 collective-permute-done.2
  15.6 1.9 convert_multiply_fusion
  17.6 4.3 fusion.135
  21.9 4.5 all-to-all-start
  26.6 12.4 %fusion.132 = (f32[400,1,1600]{2,0,1:T(8,128)S(1)}, f32[400,1,1600]{2,0,1:T(8,128)}) fusion(s32[400]{0:T(512)S(1)} %copy-done.1), kind=kLoop, calls=%fused_computation.236 | loop fusion | flops 6400000 | bytes 5121600 | tf_op jit(solution)/shard_map/cos | solution.py:36
  39.0 8.4 %all-to-all-done = f32[4,200,400]{2,1,0:T(8,128)} async-done(((f32[4,200,400]{2,1,0:T(8,128)}), f32[4,200,400]{2,1,0:T(8,128)}, u32[]{:S(2)}, u32[]{:S(2)}) %all-to-all-start) | async-done | bytes 1280032 | tf_op jit(solution)/shard_map/all_to_all | solution.py:127
  47.4 3.7 copy.22
  51.1 3.2 reshape.1089
  54.2 6.8 fusion.139
  62.5 5.1 all-to-all-start.1
  68.2 20.3 %all-to-all-done.1 = f32[400,2,1,200]{3,1,2,0:T(2,128)S(1)} async-done(((f32[400,2,1,200]{3,1,2,0:T(2,128)}), f32[400,2,1,200]{3,1,2,0:T(2,128)S(1)}, u32[]{:S(2)}, u32[]{:S(2)}) %all-to-all-start.1) | async-done | bytes 640032 | tf_op jit(solution)/shard_map/all_to_all | solution.py:132
  90.0 724.9 %while.24 = (s32[]{:T(128)}, f32[100,800]{1,0:T(8,128)S(1)}, f32[100,800]{1,0:T(8,128)S(1)}, f32[100,800]{1,0:T(8,128)S(1)}, f32[1,100,2,400]{3,2,1,0:T(2,128)S(...) while((s32[]{:T(128)}, f32[100,800]{1,0:T(8,128)S(1)}, ...), condition=%wide.region_2.3_spmd.clone.clone, body=%wide.region_1.2_spmd.clone.clone.sunk | while | flops 44908968 | bytes 40665256 | solution.py:112
  94.6 8.2 %fusion.153 = f32[1,100,2,16]{3,2,1,0:T(2,128)S(1)} fusion(f32[100,16,800]{2,0,1:T(8,128)S(1)} %multiply_multiply_fusion.34, f32[100,2,1,800]{3,1,0,2:T(2,128)S(1)} %get-tuple-element.740), kind=kOutput, calls=%fused_computation.4.clone.1 | convolution fusion | flops 30720000 | bytes 5772800 | tf_op jit(solution)/shard_map/while/body/eval_jaxpr/stj,scij->isct/dot_general | solution.py:140
  102.8 5.4 dynamic_update_slice.14
  112.7 8.2 %fusion.153 = f32[1,100,2,16]{3,2,1,0:T(2,128)S(1)} fusion(f32[100,16,800]{2,0,1:T(8,128)S(1)} %multiply_multiply_fusion.34, f32[100,2,1,800]{3,1,0,2:T(2,128)S(1)} %get-tuple-element.740), kind=kOutput, calls=%fused_computation.4.clone.1 | convolution fusion | flops 30720000 | bytes 5772800 | tf_op jit(solution)/shard_map/while/body/eval_jaxpr/stj,scij->isct/dot_general | solution.py:140
  120.9 18.4 %dynamic_update_slice.14 = f32[1,100,2,400]{3,2,1,0:T(2,128)S(1)} dynamic-update-slice(f32[1,100,2,400]{3,2,1,0:T(2,128)S(1)} %get-tuple-element.711, f32[1,100,2,16]{3,2,1,0:T(2,128)S(1)} %fusion.153, s32[]{:T(128)} %constant.302.clone.1..sunk, s32[]{:T(128)} %constant.302.clone.1..sunk, s32[]{:T(128)} %constant.302.clone.1..sunk, s32[]{:T(128)S(6)} %select_n.52) | dynamic-update-slice | bytes 25604 | tf_op jit(solution)/shard_map/while/body/eval_jaxpr/dynamic_update_slice | solution.py:109
  143.8 8.2 %fusion.153 = f32[1,100,2,16]{3,2,1,0:T(2,128)S(1)} fusion(f32[100,16,800]{2,0,1:T(8,128)S(1)} %multiply_multiply_fusion.34, f32[100,2,1,800]{3,1,0,2:T(2,128)S(1)} %get-tuple-element.740), kind=kOutput, calls=%fused_computation.4.clone.1 | convolution fusion | flops 30720000 | bytes 5772800 | tf_op jit(solution)/shard_map/while/body/eval_jaxpr/stj,scij->isct/dot_general | solution.py:140
  152.0 18.4 %dynamic_update_slice.14 = f32[1,100,2,400]{3,2,1,0:T(2,128)S(1)} dynamic-update-slice(f32[1,100,2,400]{3,2,1,0:T(2,128)S(1)} %get-tuple-element.711, f32[1,100,2,16]{3,2,1,0:T(2,128)S(1)} %fusion.153, s32[]{:T(128)} %constant.302.clone.1..sunk, s32[]{:T(128)} %constant.302.clone.1..sunk, s32[]{:T(128)} %constant.302.clone.1..sunk, s32[]{:T(128)S(6)} %select_n.52) | dynamic-update-slice | bytes 25604 | tf_op jit(solution)/shard_map/while/body/eval_jaxpr/dynamic_update_slice | solution.py:109
  174.9 8.2 %fusion.153 = f32[1,100,2,16]{3,2,1,0:T(2,128)S(1)} fusion(f32[100,16,800]{2,0,1:T(8,128)S(1)} %multiply_multiply_fusion.34, f32[100,2,1,800]{3,1,0,2:T(2,128)S(1)} %get-tuple-element.740), kind=kOutput, calls=%fused_computation.4.clone.1 | convolution fusion | flops 30720000 | bytes 5772800 | tf_op jit(solution)/shard_map/while/body/eval_jaxpr/stj,scij->isct/dot_general | solution.py:140
  183.1 18.4 %dynamic_update_slice.14 = f32[1,100,2,400]{3,2,1,0:T(2,128)S(1)} dynamic-update-slice(f32[1,100,2,400]{3,2,1,0:T(2,128)S(1)} %get-tuple-element.711, f32[1,100,2,16]{3,2,1,0:T(2,128)S(1)} %fusion.153, s32[]{:T(128)} %constant.302.clone.1..sunk, s32[]{:T(128)} %constant.302.clone.1..sunk, s32[]{:T(128)} %constant.302.clone.1..sunk, s32[]{:T(128)S(6)} %select_n.52) | dynamic-update-slice | bytes 25604 | tf_op jit(solution)/shard_map/while/body/eval_jaxpr/dynamic_update_slice | solution.py:109
  206.0 8.2 %fusion.153 = f32[1,100,2,16]{3,2,1,0:T(2,128)S(1)} fusion(f32[100,16,800]{2,0,1:T(8,128)S(1)} %multiply_multiply_fusion.34, f32[100,2,1,800]{3,1,0,2:T(2,128)S(1)} %get-tuple-element.740), kind=kOutput, calls=%fused_computation.4.clone.1 | convolution fusion | flops 30720000 | bytes 5772800 | tf_op jit(solution)/shard_map/while/body/eval_jaxpr/stj,scij->isct/dot_general | solution.py:140
  214.2 18.4 %dynamic_update_slice.14 = f32[1,100,2,400]{3,2,1,0:T(2,128)S(1)} dynamic-update-slice(f32[1,100,2,400]{3,2,1,0:T(2,128)S(1)} %get-tuple-element.711, f32[1,100,2,16]{3,2,1,0:T(2,128)S(1)} %fusion.153, s32[]{:T(128)} %constant.302.clone.1..sunk, s32[]{:T(128)} %constant.302.clone.1..sunk, s32[]{:T(128)} %constant.302.clone.1..sunk, s32[]{:T(128)S(6)} %select_n.52) | dynamic-update-slice | bytes 25604 | tf_op jit(solution)/shard_map/while/body/eval_jaxpr/dynamic_update_slice | solution.py:109
  237.1 8.2 %fusion.153 = f32[1,100,2,16]{3,2,1,0:T(2,128)S(1)} fusion(f32[100,16,800]{2,0,1:T(8,128)S(1)} %multiply_multiply_fusion.34, f32[100,2,1,800]{3,1,0,2:T(2,128)S(1)} %get-tuple-element.740), kind=kOutput, calls=%fused_computation.4.clone.1 | convolution fusion | flops 30720000 | bytes 5772800 | tf_op jit(solution)/shard_map/while/body/eval_jaxpr/stj,scij->isct/dot_general | solution.py:140
  245.3 18.4 %dynamic_update_slice.14 = f32[1,100,2,400]{3,2,1,0:T(2,128)S(1)} dynamic-update-slice(f32[1,100,2,400]{3,2,1,0:T(2,128)S(1)} %get-tuple-element.711, f32[1,100,2,16]{3,2,1,0:T(2,128)S(1)} %fusion.153, s32[]{:T(128)} %constant.302.clone.1..sunk, s32[]{:T(128)} %constant.302.clone.1..sunk, s32[]{:T(128)} %constant.302.clone.1..sunk, s32[]{:T(128)S(6)} %select_n.52) | dynamic-update-slice | bytes 25604 | tf_op jit(solution)/shard_map/while/body/eval_jaxpr/dynamic_update_slice | solution.py:109
  268.2 8.2 %fusion.153 = f32[1,100,2,16]{3,2,1,0:T(2,128)S(1)} fusion(f32[100,16,800]{2,0,1:T(8,128)S(1)} %multiply_multiply_fusion.34, f32[100,2,1,800]{3,1,0,2:T(2,128)S(1)} %get-tuple-element.740), kind=kOutput, calls=%fused_computation.4.clone.1 | convolution fusion | flops 30720000 | bytes 5772800 | tf_op jit(solution)/shard_map/while/body/eval_jaxpr/stj,scij->isct/dot_general | solution.py:140
  276.3 18.4 %dynamic_update_slice.14 = f32[1,100,2,400]{3,2,1,0:T(2,128)S(1)} dynamic-update-slice(f32[1,100,2,400]{3,2,1,0:T(2,128)S(1)} %get-tuple-element.711, f32[1,100,2,16]{3,2,1,0:T(2,128)S(1)} %fusion.153, s32[]{:T(128)} %constant.302.clone.1..sunk, s32[]{:T(128)} %constant.302.clone.1..sunk, s32[]{:T(128)} %constant.302.clone.1..sunk, s32[]{:T(128)S(6)} %select_n.52) | dynamic-update-slice | bytes 25604 | tf_op jit(solution)/shard_map/while/body/eval_jaxpr/dynamic_update_slice | solution.py:109
  299.3 8.2 %fusion.153 = f32[1,100,2,16]{3,2,1,0:T(2,128)S(1)} fusion(f32[100,16,800]{2,0,1:T(8,128)S(1)} %multiply_multiply_fusion.34, f32[100,2,1,800]{3,1,0,2:T(2,128)S(1)} %get-tuple-element.740), kind=kOutput, calls=%fused_computation.4.clone.1 | convolution fusion | flops 30720000 | bytes 5772800 | tf_op jit(solution)/shard_map/while/body/eval_jaxpr/stj,scij->isct/dot_general | solution.py:140
  307.4 18.4 %dynamic_update_slice.14 = f32[1,100,2,400]{3,2,1,0:T(2,128)S(1)} dynamic-update-slice(f32[1,100,2,400]{3,2,1,0:T(2,128)S(1)} %get-tuple-element.711, f32[1,100,2,16]{3,2,1,0:T(2,128)S(1)} %fusion.153, s32[]{:T(128)} %constant.302.clone.1..sunk, s32[]{:T(128)} %constant.302.clone.1..sunk, s32[]{:T(128)} %constant.302.clone.1..sunk, s32[]{:T(128)S(6)} %select_n.52) | dynamic-update-slice | bytes 25604 | tf_op jit(solution)/shard_map/while/body/eval_jaxpr/dynamic_update_slice | solution.py:109
  330.4 8.2 %fusion.153 = f32[1,100,2,16]{3,2,1,0:T(2,128)S(1)} fusion(f32[100,16,800]{2,0,1:T(8,128)S(1)} %multiply_multiply_fusion.34, f32[100,2,1,800]{3,1,0,2:T(2,128)S(1)} %get-tuple-element.740), kind=kOutput, calls=%fused_computation.4.clone.1 | convolution fusion | flops 30720000 | bytes 5772800 | tf_op jit(solution)/shard_map/while/body/eval_jaxpr/stj,scij->isct/dot_general | solution.py:140
  338.5 5.4 dynamic_update_slice.14
  348.4 8.2 %fusion.153 = f32[1,100,2,16]{3,2,1,0:T(2,128)S(1)} fusion(f32[100,16,800]{2,0,1:T(8,128)S(1)} %multiply_multiply_fusion.34, f32[100,2,1,800]{3,1,0,2:T(2,128)S(1)} %get-tuple-element.740), kind=kOutput, calls=%fused_computation.4.clone.1 | convolution fusion | flops 30720000 | bytes 5772800 | tf_op jit(solution)/shard_map/while/body/eval_jaxpr/stj,scij->isct/dot_general | solution.py:140
  356.6 18.4 %dynamic_update_slice.14 = f32[1,100,2,400]{3,2,1,0:T(2,128)S(1)} dynamic-update-slice(f32[1,100,2,400]{3,2,1,0:T(2,128)S(1)} %get-tuple-element.711, f32[1,100,2,16]{3,2,1,0:T(2,128)S(1)} %fusion.153, s32[]{:T(128)} %constant.302.clone.1..sunk, s32[]{:T(128)} %constant.302.clone.1..sunk, s32[]{:T(128)} %constant.302.clone.1..sunk, s32[]{:T(128)S(6)} %select_n.52) | dynamic-update-slice | bytes 25604 | tf_op jit(solution)/shard_map/while/body/eval_jaxpr/dynamic_update_slice | solution.py:109
  379.5 8.2 %fusion.153 = f32[1,100,2,16]{3,2,1,0:T(2,128)S(1)} fusion(f32[100,16,800]{2,0,1:T(8,128)S(1)} %multiply_multiply_fusion.34, f32[100,2,1,800]{3,1,0,2:T(2,128)S(1)} %get-tuple-element.740), kind=kOutput, calls=%fused_computation.4.clone.1 | convolution fusion | flops 30720000 | bytes 5772800 | tf_op jit(solution)/shard_map/while/body/eval_jaxpr/stj,scij->isct/dot_general | solution.py:140
  387.7 18.4 %dynamic_update_slice.14 = f32[1,100,2,400]{3,2,1,0:T(2,128)S(1)} dynamic-update-slice(f32[1,100,2,400]{3,2,1,0:T(2,128)S(1)} %get-tuple-element.711, f32[1,100,2,16]{3,2,1,0:T(2,128)S(1)} %fusion.153, s32[]{:T(128)} %constant.302.clone.1..sunk, s32[]{:T(128)} %constant.302.clone.1..sunk, s32[]{:T(128)} %constant.302.clone.1..sunk, s32[]{:T(128)S(6)} %select_n.52) | dynamic-update-slice | bytes 25604 | tf_op jit(solution)/shard_map/while/body/eval_jaxpr/dynamic_update_slice | solution.py:109
  410.6 8.2 %fusion.153 = f32[1,100,2,16]{3,2,1,0:T(2,128)S(1)} fusion(f32[100,16,800]{2,0,1:T(8,128)S(1)} %multiply_multiply_fusion.34, f32[100,2,1,800]{3,1,0,2:T(2,128)S(1)} %get-tuple-element.740), kind=kOutput, calls=%fused_computation.4.clone.1 | convolution fusion | flops 30720000 | bytes 5772800 | tf_op jit(solution)/shard_map/while/body/eval_jaxpr/stj,scij->isct/dot_general | solution.py:140
  418.8 18.4 %dynamic_update_slice.14 = f32[1,100,2,400]{3,2,1,0:T(2,128)S(1)} dynamic-update-slice(f32[1,100,2,400]{3,2,1,0:T(2,128)S(1)} %get-tuple-element.711, f32[1,100,2,16]{3,2,1,0:T(2,128)S(1)} %fusion.153, s32[]{:T(128)} %constant.302.clone.1..sunk, s32[]{:T(128)} %constant.302.clone.1..sunk, s32[]{:T(128)} %constant.302.clone.1..sunk, s32[]{:T(128)S(6)} %select_n.52) | dynamic-update-slice | bytes 25604 | tf_op jit(solution)/shard_map/while/body/eval_jaxpr/dynamic_update_slice | solution.py:109
  441.7 8.2 %fusion.153 = f32[1,100,2,16]{3,2,1,0:T(2,128)S(1)} fusion(f32[100,16,800]{2,0,1:T(8,128)S(1)} %multiply_multiply_fusion.34, f32[100,2,1,800]{3,1,0,2:T(2,128)S(1)} %get-tuple-element.740), kind=kOutput, calls=%fused_computation.4.clone.1 | convolution fusion | flops 30720000 | bytes 5772800 | tf_op jit(solution)/shard_map/while/body/eval_jaxpr/stj,scij->isct/dot_general | solution.py:140
  449.9 18.4 %dynamic_update_slice.14 = f32[1,100,2,400]{3,2,1,0:T(2,128)S(1)} dynamic-update-slice(f32[1,100,2,400]{3,2,1,0:T(2,128)S(1)} %get-tuple-element.711, f32[1,100,2,16]{3,2,1,0:T(2,128)S(1)} %fusion.153, s32[]{:T(128)} %constant.302.clone.1..sunk, s32[]{:T(128)} %constant.302.clone.1..sunk, s32[]{:T(128)} %constant.302.clone.1..sunk, s32[]{:T(128)S(6)} %select_n.52) | dynamic-update-slice | bytes 25604 | tf_op jit(solution)/shard_map/while/body/eval_jaxpr/dynamic_update_slice | solution.py:109
  472.8 8.2 %fusion.153 = f32[1,100,2,16]{3,2,1,0:T(2,128)S(1)} fusion(f32[100,16,800]{2,0,1:T(8,128)S(1)} %multiply_multiply_fusion.34, f32[100,2,1,800]{3,1,0,2:T(2,128)S(1)} %get-tuple-element.740), kind=kOutput, calls=%fused_computation.4.clone.1 | convolution fusion | flops 30720000 | bytes 5772800 | tf_op jit(solution)/shard_map/while/body/eval_jaxpr/stj,scij->isct/dot_general | solution.py:140
  481.0 18.4 %dynamic_update_slice.14 = f32[1,100,2,400]{3,2,1,0:T(2,128)S(1)} dynamic-update-slice(f32[1,100,2,400]{3,2,1,0:T(2,128)S(1)} %get-tuple-element.711, f32[1,100,2,16]{3,2,1,0:T(2,128)S(1)} %fusion.153, s32[]{:T(128)} %constant.302.clone.1..sunk, s32[]{:T(128)} %constant.302.clone.1..sunk, s32[]{:T(128)} %constant.302.clone.1..sunk, s32[]{:T(128)S(6)} %select_n.52) | dynamic-update-slice | bytes 25604 | tf_op jit(solution)/shard_map/while/body/eval_jaxpr/dynamic_update_slice | solution.py:109
  503.9 8.2 %fusion.153 = f32[1,100,2,16]{3,2,1,0:T(2,128)S(1)} fusion(f32[100,16,800]{2,0,1:T(8,128)S(1)} %multiply_multiply_fusion.34, f32[100,2,1,800]{3,1,0,2:T(2,128)S(1)} %get-tuple-element.740), kind=kOutput, calls=%fused_computation.4.clone.1 | convolution fusion | flops 30720000 | bytes 5772800 | tf_op jit(solution)/shard_map/while/body/eval_jaxpr/stj,scij->isct/dot_general | solution.py:140
  512.1 18.4 %dynamic_update_slice.14 = f32[1,100,2,400]{3,2,1,0:T(2,128)S(1)} dynamic-update-slice(f32[1,100,2,400]{3,2,1,0:T(2,128)S(1)} %get-tuple-element.711, f32[1,100,2,16]{3,2,1,0:T(2,128)S(1)} %fusion.153, s32[]{:T(128)} %constant.302.clone.1..sunk, s32[]{:T(128)} %constant.302.clone.1..sunk, s32[]{:T(128)} %constant.302.clone.1..sunk, s32[]{:T(128)S(6)} %select_n.52) | dynamic-update-slice | bytes 25604 | tf_op jit(solution)/shard_map/while/body/eval_jaxpr/dynamic_update_slice | solution.py:109
  535.0 8.2 %fusion.153 = f32[1,100,2,16]{3,2,1,0:T(2,128)S(1)} fusion(f32[100,16,800]{2,0,1:T(8,128)S(1)} %multiply_multiply_fusion.34, f32[100,2,1,800]{3,1,0,2:T(2,128)S(1)} %get-tuple-element.740), kind=kOutput, calls=%fused_computation.4.clone.1 | convolution fusion | flops 30720000 | bytes 5772800 | tf_op jit(solution)/shard_map/while/body/eval_jaxpr/stj,scij->isct/dot_general | solution.py:140
  543.2 18.4 %dynamic_update_slice.14 = f32[1,100,2,400]{3,2,1,0:T(2,128)S(1)} dynamic-update-slice(f32[1,100,2,400]{3,2,1,0:T(2,128)S(1)} %get-tuple-element.711, f32[1,100,2,16]{3,2,1,0:T(2,128)S(1)} %fusion.153, s32[]{:T(128)} %constant.302.clone.1..sunk, s32[]{:T(128)} %constant.302.clone.1..sunk, s32[]{:T(128)} %constant.302.clone.1..sunk, s32[]{:T(128)S(6)} %select_n.52) | dynamic-update-slice | bytes 25604 | tf_op jit(solution)/shard_map/while/body/eval_jaxpr/dynamic_update_slice | solution.py:109
  566.1 8.2 %fusion.153 = f32[1,100,2,16]{3,2,1,0:T(2,128)S(1)} fusion(f32[100,16,800]{2,0,1:T(8,128)S(1)} %multiply_multiply_fusion.34, f32[100,2,1,800]{3,1,0,2:T(2,128)S(1)} %get-tuple-element.740), kind=kOutput, calls=%fused_computation.4.clone.1 | convolution fusion | flops 30720000 | bytes 5772800 | tf_op jit(solution)/shard_map/while/body/eval_jaxpr/stj,scij->isct/dot_general | solution.py:140
  574.3 5.4 dynamic_update_slice.14
  584.1 8.2 %fusion.153 = f32[1,100,2,16]{3,2,1,0:T(2,128)S(1)} fusion(f32[100,16,800]{2,0,1:T(8,128)S(1)} %multiply_multiply_fusion.34, f32[100,2,1,800]{3,1,0,2:T(2,128)S(1)} %get-tuple-element.740), kind=kOutput, calls=%fused_computation.4.clone.1 | convolution fusion | flops 30720000 | bytes 5772800 | tf_op jit(solution)/shard_map/while/body/eval_jaxpr/stj,scij->isct/dot_general | solution.py:140
  592.3 18.4 %dynamic_update_slice.14 = f32[1,100,2,400]{3,2,1,0:T(2,128)S(1)} dynamic-update-slice(f32[1,100,2,400]{3,2,1,0:T(2,128)S(1)} %get-tuple-element.711, f32[1,100,2,16]{3,2,1,0:T(2,128)S(1)} %fusion.153, s32[]{:T(128)} %constant.302.clone.1..sunk, s32[]{:T(128)} %constant.302.clone.1..sunk, s32[]{:T(128)} %constant.302.clone.1..sunk, s32[]{:T(128)S(6)} %select_n.52) | dynamic-update-slice | bytes 25604 | tf_op jit(solution)/shard_map/while/body/eval_jaxpr/dynamic_update_slice | solution.py:109
  615.2 8.2 %fusion.153 = f32[1,100,2,16]{3,2,1,0:T(2,128)S(1)} fusion(f32[100,16,800]{2,0,1:T(8,128)S(1)} %multiply_multiply_fusion.34, f32[100,2,1,800]{3,1,0,2:T(2,128)S(1)} %get-tuple-element.740), kind=kOutput, calls=%fused_computation.4.clone.1 | convolution fusion | flops 30720000 | bytes 5772800 | tf_op jit(solution)/shard_map/while/body/eval_jaxpr/stj,scij->isct/dot_general | solution.py:140
  623.4 18.4 %dynamic_update_slice.14 = f32[1,100,2,400]{3,2,1,0:T(2,128)S(1)} dynamic-update-slice(f32[1,100,2,400]{3,2,1,0:T(2,128)S(1)} %get-tuple-element.711, f32[1,100,2,16]{3,2,1,0:T(2,128)S(1)} %fusion.153, s32[]{:T(128)} %constant.302.clone.1..sunk, s32[]{:T(128)} %constant.302.clone.1..sunk, s32[]{:T(128)} %constant.302.clone.1..sunk, s32[]{:T(128)S(6)} %select_n.52) | dynamic-update-slice | bytes 25604 | tf_op jit(solution)/shard_map/while/body/eval_jaxpr/dynamic_update_slice | solution.py:109
  646.3 8.2 %fusion.153 = f32[1,100,2,16]{3,2,1,0:T(2,128)S(1)} fusion(f32[100,16,800]{2,0,1:T(8,128)S(1)} %multiply_multiply_fusion.34, f32[100,2,1,800]{3,1,0,2:T(2,128)S(1)} %get-tuple-element.740), kind=kOutput, calls=%fused_computation.4.clone.1 | convolution fusion | flops 30720000 | bytes 5772800 | tf_op jit(solution)/shard_map/while/body/eval_jaxpr/stj,scij->isct/dot_general | solution.py:140
  654.5 18.4 %dynamic_update_slice.14 = f32[1,100,2,400]{3,2,1,0:T(2,128)S(1)} dynamic-update-slice(f32[1,100,2,400]{3,2,1,0:T(2,128)S(1)} %get-tuple-element.711, f32[1,100,2,16]{3,2,1,0:T(2,128)S(1)} %fusion.153, s32[]{:T(128)} %constant.302.clone.1..sunk, s32[]{:T(128)} %constant.302.clone.1..sunk, s32[]{:T(128)} %constant.302.clone.1..sunk, s32[]{:T(128)S(6)} %select_n.52) | dynamic-update-slice | bytes 25604 | tf_op jit(solution)/shard_map/while/body/eval_jaxpr/dynamic_update_slice | solution.py:109
  677.4 8.2 %fusion.153 = f32[1,100,2,16]{3,2,1,0:T(2,128)S(1)} fusion(f32[100,16,800]{2,0,1:T(8,128)S(1)} %multiply_multiply_fusion.34, f32[100,2,1,800]{3,1,0,2:T(2,128)S(1)} %get-tuple-element.740), kind=kOutput, calls=%fused_computation.4.clone.1 | convolution fusion | flops 30720000 | bytes 5772800 | tf_op jit(solution)/shard_map/while/body/eval_jaxpr/stj,scij->isct/dot_general | solution.py:140
  685.6 18.4 %dynamic_update_slice.14 = f32[1,100,2,400]{3,2,1,0:T(2,128)S(1)} dynamic-update-slice(f32[1,100,2,400]{3,2,1,0:T(2,128)S(1)} %get-tuple-element.711, f32[1,100,2,16]{3,2,1,0:T(2,128)S(1)} %fusion.153, s32[]{:T(128)} %constant.302.clone.1..sunk, s32[]{:T(128)} %constant.302.clone.1..sunk, s32[]{:T(128)} %constant.302.clone.1..sunk, s32[]{:T(128)S(6)} %select_n.52) | dynamic-update-slice | bytes 25604 | tf_op jit(solution)/shard_map/while/body/eval_jaxpr/dynamic_update_slice | solution.py:109
  708.5 8.2 %fusion.153 = f32[1,100,2,16]{3,2,1,0:T(2,128)S(1)} fusion(f32[100,16,800]{2,0,1:T(8,128)S(1)} %multiply_multiply_fusion.34, f32[100,2,1,800]{3,1,0,2:T(2,128)S(1)} %get-tuple-element.740), kind=kOutput, calls=%fused_computation.4.clone.1 | convolution fusion | flops 30720000 | bytes 5772800 | tf_op jit(solution)/shard_map/while/body/eval_jaxpr/stj,scij->isct/dot_general | solution.py:140
  716.7 18.4 %dynamic_update_slice.14 = f32[1,100,2,400]{3,2,1,0:T(2,128)S(1)} dynamic-update-slice(f32[1,100,2,400]{3,2,1,0:T(2,128)S(1)} %get-tuple-element.711, f32[1,100,2,16]{3,2,1,0:T(2,128)S(1)} %fusion.153, s32[]{:T(128)} %constant.302.clone.1..sunk, s32[]{:T(128)} %constant.302.clone.1..sunk, s32[]{:T(128)} %constant.302.clone.1..sunk, s32[]{:T(128)S(6)} %select_n.52) | dynamic-update-slice | bytes 25604 | tf_op jit(solution)/shard_map/while/body/eval_jaxpr/dynamic_update_slice | solution.py:109
  739.6 8.2 %fusion.153 = f32[1,100,2,16]{3,2,1,0:T(2,128)S(1)} fusion(f32[100,16,800]{2,0,1:T(8,128)S(1)} %multiply_multiply_fusion.34, f32[100,2,1,800]{3,1,0,2:T(2,128)S(1)} %get-tuple-element.740), kind=kOutput, calls=%fused_computation.4.clone.1 | convolution fusion | flops 30720000 | bytes 5772800 | tf_op jit(solution)/shard_map/while/body/eval_jaxpr/stj,scij->isct/dot_general | solution.py:140
  747.8 18.4 %dynamic_update_slice.14 = f32[1,100,2,400]{3,2,1,0:T(2,128)S(1)} dynamic-update-slice(f32[1,100,2,400]{3,2,1,0:T(2,128)S(1)} %get-tuple-element.711, f32[1,100,2,16]{3,2,1,0:T(2,128)S(1)} %fusion.153, s32[]{:T(128)} %constant.302.clone.1..sunk, s32[]{:T(128)} %constant.302.clone.1..sunk, s32[]{:T(128)} %constant.302.clone.1..sunk, s32[]{:T(128)S(6)} %select_n.52) | dynamic-update-slice | bytes 25604 | tf_op jit(solution)/shard_map/while/body/eval_jaxpr/dynamic_update_slice | solution.py:109
  770.7 8.2 %fusion.153 = f32[1,100,2,16]{3,2,1,0:T(2,128)S(1)} fusion(f32[100,16,800]{2,0,1:T(8,128)S(1)} %multiply_multiply_fusion.34, f32[100,2,1,800]{3,1,0,2:T(2,128)S(1)} %get-tuple-element.740), kind=kOutput, calls=%fused_computation.4.clone.1 | convolution fusion | flops 30720000 | bytes 5772800 | tf_op jit(solution)/shard_map/while/body/eval_jaxpr/stj,scij->isct/dot_general | solution.py:140
  778.9 18.4 %dynamic_update_slice.14 = f32[1,100,2,400]{3,2,1,0:T(2,128)S(1)} dynamic-update-slice(f32[1,100,2,400]{3,2,1,0:T(2,128)S(1)} %get-tuple-element.711, f32[1,100,2,16]{3,2,1,0:T(2,128)S(1)} %fusion.153, s32[]{:T(128)} %constant.302.clone.1..sunk, s32[]{:T(128)} %constant.302.clone.1..sunk, s32[]{:T(128)} %constant.302.clone.1..sunk, s32[]{:T(128)S(6)} %select_n.52) | dynamic-update-slice | bytes 25604 | tf_op jit(solution)/shard_map/while/body/eval_jaxpr/dynamic_update_slice | solution.py:109
  801.8 8.2 %fusion.153 = f32[1,100,2,16]{3,2,1,0:T(2,128)S(1)} fusion(f32[100,16,800]{2,0,1:T(8,128)S(1)} %multiply_multiply_fusion.34, f32[100,2,1,800]{3,1,0,2:T(2,128)S(1)} %get-tuple-element.740), kind=kOutput, calls=%fused_computation.4.clone.1 | convolution fusion | flops 30720000 | bytes 5772800 | tf_op jit(solution)/shard_map/while/body/eval_jaxpr/stj,scij->isct/dot_general | solution.py:140
  810.0 4.9 dynamic_update_slice.14
  (579 shorter events, 118.7 us)
Async XLA Ops:
  0.8 6.8 collective-permute-start
  3.9 3.7 collective-permute-start.1
  8.9 5.7 collective-permute-start.2
  9.0 6.7 collective-permute-start.3
  17.5 8.9 %copy-start.1 = (s32[400]{0:T(512)S(1)}, s32[400]{0:T(512)}, u32[]{:S(2)}) copy-start(s32[400]{0:T(512)} %param.11) | copy-start | bytes 4804
  17.5 8.9 %copy-start.2 = (s32[200]{0:T(256)S(1)}, s32[200]{0:T(256)}, u32[]{:S(2)}) copy-start(s32[200]{0:T(256)} %param.10) | copy-start | bytes 2404
  21.9 25.5 %all-to-all-start = ((f32[4,200,400]{2,1,0:T(8,128)}), f32[4,200,400]{2,1,0:T(8,128)}, u32[]{:S(2)}, u32[]{:S(2)}) async-start(f32[4,200,400]{2,1,0:T(8,128)} %fusion.135), calls=%async_computation | async-start | bytes 3276800 | tf_op jit(solution)/shard_map/all_to_all | solution.py:127
  62.5 25.9 %all-to-all-start.1 = ((f32[400,2,1,200]{3,1,2,0:T(2,128)}), f32[400,2,1,200]{3,1,2,0:T(2,128)S(1)}, u32[]{:S(2)}, u32[]{:S(2)}) async-start(f32[400,2,1,200]{3,1,2,0:T(2,128)} %copy.23), calls=%async_computation.1 | async-start | bytes 1638400 | tf_op jit(solution)/shard_map/all_to_all | solution.py:132
  814.9 0.8 copy-start
where the time goes:
time: 816 us
  local copies, waits for them, and re-layouts  419 us (51%)
  matrix products  211 us (26%)
  other arithmetic  129 us (16%)
  waiting for transfers between devices  35.3 us (4%)
  starting transfers between devices  16.6 us (2%)
    dynamic_update_slice x25, local copies, waits for them, and re-layouts, advance(): lax.dynamic_update_slice_in_dim(result_now, partial_value, first_order, 3)  408 us
    dot_general x25, matrix products, contract(): return jnp.einsum('stj,scij->isct', table_rows, weighted, precision=precise)  205 us
    while x375, other arithmetic  72.1 us
    all_to_all x1, waiting for transfers between devices, shards(): lax.all_to_all(fourier, 'lat', split_axis=0, concat_axis=3, tiled=True)  20.3 us
  transfers between devices with their start and end apart: 6, of which 5 were waited for; matrix products, arithmetic and copies ran while one was open for 2% of the time, Pallas kernels for 0%

commit v1 on v0

v1 whole, which is shorter than its diff:
```python
import math

import jax
import jax.numpy as jnp
from jax import lax
from jax.experimental import pallas as pl
from jax.experimental.pallas import tpu as pltpu
from jax.sharding import PartitionSpec as P

M = 400
NLAT = 800
NLON = 1600

block_rows = 16
slot_tile = 16
GROUP = ("lev", "fld")


def round_up(value, multiple):
    return -(-value // multiple) * multiple


def edges(block, axis, dim):
    count = lax.axis_size(axis)
    forward = [(i, (i + 1) % count) for i in range(count)]
    backward = [(target, source) for source, target in forward]
    low = lax.ppermute(
        lax.slice_in_dim(block, block.shape[dim] - 1, None, axis=dim), axis, forward
    )
    high = lax.ppermute(lax.slice_in_dim(block, 0, 1, axis=dim), axis, backward)
    return low, high


def fourier_table(wave_ids, lon_count):
    grid_index = jnp.arange(lon_count, dtype=jnp.int32)
    phase_index = wave_ids[:, None] * grid_index[None, :] % lon_count
    angles = 2.0 * math.pi / lon_count * phase_index.astype(jnp.float32)
    factor = 1.0 / math.sqrt(lon_count)
    return jnp.stack([jnp.cos(angles), -jnp.sin(angles)], axis=1) * factor


def advect(tracer, east_wind, north_wind, first_row, lat_total):
    west, east = edges(tracer, GROUP, 2)
    above, below = edges(tracer, "lat", 1)
    centre = tracer.astype(jnp.float32)
    rows_here = tracer.shape[1]
    has_above = (first_row > 0).astype(jnp.float32)
    has_below = (first_row + rows_here < lat_total).astype(jnp.float32)
    above = above.astype(jnp.float32) * has_above
    below = below.astype(jnp.float32) * has_below
    east_diff = jnp.concatenate(
        [centre[:, :, 1:], east.astype(jnp.float32)], axis=2
    ) - jnp.concatenate([west.astype(jnp.float32), centre[:, :, :-1]], axis=2)
    north_diff = jnp.concatenate([centre[:, 1:], below], axis=1) - jnp.concatenate(
        [above, centre[:, :-1]], axis=1
    )
    return (
        centre
        - 0.5 * east_wind.astype(jnp.float32) * east_diff
        - 0.5 * north_wind.astype(jnp.float32) * north_diff
    )


def legendre_setup(wave_ids, trunc_count, lat_total, lat_used, lat_padded):
    degree = jnp.minimum(wave_ids, trunc_count - 1).astype(jnp.float32)
    counter = jnp.arange(1, trunc_count, dtype=jnp.float32)
    log_terms = jnp.log1p(0.5 / counter)
    log_norm = jnp.sum(
        jnp.where(counter[None, :] <= degree[:, None], log_terms[None, :], 0.0), axis=1
    )
    rows = jnp.minimum(jnp.arange(lat_padded), lat_used - 1)
    colatitude = math.pi / lat_total * (rows.astype(jnp.float32) + 0.5)
    start_log = 0.5 * (log_norm[:, None] - math.log(2.0)) + degree[:, None] * jnp.log(
        jnp.sin(colatitude)
    )
    orders = jnp.arange(1, trunc_count + 1, dtype=jnp.float32)
    total = degree[:, None] + orders
    square = degree[:, None] * degree[:, None]
    growth = jnp.sqrt((4.0 * total * total - 1.0) / (total * total - square))
    lower = total - 1.0
    damping = jnp.sqrt(
        (lower * lower - square) / jnp.maximum(4.0 * lower * lower - 1.0, 1.0)
    )

    def blocked(values):
        return values.reshape(values.shape[0], -1, block_rows).transpose(1, 0, 2)

    return blocked(growth), blocked(damping), jnp.cos(colatitude)[None, :], start_log


def table_kernel(growth_ref, damping_ref, cosine_ref, start_ref, high_ref, low_ref):
    cosine = cosine_ref[...]
    shape = start_ref.shape

    def advance(index, carry):
        before, current, log_scale = carry
        scale = jnp.exp(log_scale)
        growth = growth_ref[index]
        damping = damping_ref[index]
        for offset in range(block_rows):
            row = current * scale
            high = row.astype(jnp.bfloat16)
            low = (row - high.astype(jnp.float32)).astype(jnp.bfloat16)
            place = index * (block_rows // 2) + offset // 2
            high_ref[offset % 2, place] = high
            low_ref[offset % 2, place] = low
            advanced = growth[:, offset : offset + 1] * (
                cosine * current - damping[:, offset : offset + 1] * before
            )
            before, current = current, advanced
        biggest = jnp.maximum(jnp.abs(before), jnp.abs(current))
        return before / biggest, current / biggest, log_scale + jnp.log(biggest)

    lax.fori_loop(
        0,
        growth_ref.shape[0],
        advance,
        (jnp.zeros(shape, jnp.float32), jnp.ones(shape, jnp.float32), start_ref[...]),
    )


def legendre_table(growth, damping, cosine, start_log):
    blocks, slots, _ = growth.shape
    lats = cosine.shape[1]
    half = blocks * block_rows // 2
    out = jax.ShapeDtypeStruct((2, half, slots, lats), jnp.bfloat16)
    coef_spec = pl.BlockSpec((blocks, slot_tile, block_rows), lambda i: (0, i, 0))
    out_spec = pl.BlockSpec((2, half, slot_tile, lats), lambda i: (0, 0, i, 0))
    size = 2 * half * slots * lats
    return pl.pallas_call(
        table_kernel,
        grid=(slots // slot_tile,),
        in_specs=[
            coef_spec,
            coef_spec,
            pl.BlockSpec((1, lats), lambda i: (0, 0)),
            pl.BlockSpec((slot_tile, lats), lambda i: (i, 0)),
        ],
        out_specs=[out_spec, out_spec],
        out_shape=[out, out],
        cost_estimate=pl.CostEstimate(
            flops=10 * size, bytes_accessed=4 * size, transcendentals=size // 4
        ),
        name="legendre_table",
    )(growth, damping, cosine, start_log)


def contract_kernel(columns_per_slot, high_ref, low_ref, weight_high_ref, weight_low_ref, out_ref):
    _, orders, slots, lats = high_ref.shape
    columns = out_ref.shape[2]
    high = high_ref[0].reshape(orders * slots, lats)
    low = low_ref[0].reshape(orders * slots, lats)

    def dot(left, right):
        return lax.dot_general(
            left, right, (((1,), (1,)), ((), ())), preferred_element_type=jnp.float32
        )

    full = (
        dot(high, weight_high_ref[0]) + dot(high, weight_low_ref[0]) + dot(low, weight_high_ref[0])
    )
    slot_of_row = lax.broadcasted_iota(jnp.int32, (slots, columns), 0)
    column = lax.broadcasted_iota(jnp.int32, (slots, columns), 1)
    first = slot_of_row * columns_per_slot
    own = (column >= first) & (column < first + columns_per_slot)
    picked = jnp.where(own[None], full.reshape(orders, slots, columns), 0.0)
    out_ref[0] = jnp.sum(picked, axis=1)


def contract_table(high, low, weight_high, weight_low, columns_per_slot):
    _, half, slots, lats = high.shape
    columns = weight_high.shape[1]
    tile = 40
    table_spec = pl.BlockSpec((1, tile, slots, lats), lambda p, i: (p, i, 0, 0))
    weight_spec = pl.BlockSpec((1, columns, lats), lambda p, i: (p, 0, 0))
    return pl.pallas_call(
        lambda *refs: contract_kernel(columns_per_slot, *refs),
        grid=(2, half // tile),
        in_specs=[table_spec, table_spec, weight_spec, weight_spec],
        out_specs=pl.BlockSpec((1, tile, columns), lambda p, i: (p, i, 0)),
        out_shape=jax.ShapeDtypeStruct((2, half, columns), jnp.float32),
        cost_estimate=pl.CostEstimate(
            flops=12 * half * slots * lats * columns,
            bytes_accessed=8 * half * slots * lats,
            transcendentals=0,
        ),
        name="legendre_contract",
    )(high, low, weight_high, weight_low)


def split_pair(values):
    high = lax.reduce_precision(values, 8, 7)
    return high.astype(jnp.bfloat16), (values - high).astype(jnp.bfloat16)


def shards(tracer, wind_east, wind_north, keep_m, slot_wave):
    groups = lax.axis_size("lev") * lax.axis_size("fld")
    lat_parts = lax.axis_size("lat")
    levels, lat_rows, _ = tracer.shape
    own_levels = levels // groups
    slots_lat = slot_wave.shape[0] // lat_parts
    slots_own = -(-slots_lat // groups)
    first_row = lax.axis_index("lat") * lat_rows

    waves = jnp.pad(
        slot_wave.reshape(lat_parts, slots_lat),
        ((0, 0), (0, groups * slots_own - slots_lat)),
        constant_values=M,
    ).reshape(-1)
    place = lax.axis_index(("lat",) + GROUP) * slots_own
    my_waves = lax.dynamic_slice_in_dim(waves, place, slots_own)

    half_lat = NLAT // 2
    lat_padded = round_up(half_lat, 128)
    slots_padded = round_up(slots_own, slot_tile)
    padded_waves = jnp.pad(my_waves, (0, slots_padded - slots_own))
    table_high, table_low = legendre_table(
        *legendre_setup(padded_waves, M, NLAT, half_lat, lat_padded)
    )

    advected = advect(tracer, wind_east, wind_north, first_row, NLAT)
    advected = lax.all_to_all(advected, GROUP, split_axis=0, concat_axis=2, tiled=True)
    fourier = jnp.einsum(
        "sck,ijk->scij", fourier_table(waves, NLON), advected, precision=lax.Precision.HIGH
    )
    kept_mask = (waves[:, None] < keep_m[None, :]).astype(jnp.float32)
    fourier = fourier * kept_mask[:, None, None, :]
    fourier = fourier.reshape(lat_parts * groups, slots_own * 2 * own_levels, lat_rows)
    spectral_in = lax.all_to_all(
        fourier, ("lat",) + GROUP, split_axis=0, concat_axis=0, tiled=True
    )
    spectral_in = spectral_in.reshape(lat_parts, groups, slots_own, 2, own_levels, lat_rows)
    columns_per_slot = levels * 2
    used = slots_own * columns_per_slot
    weighted = spectral_in.transpose(2, 1, 4, 3, 0, 5).reshape(used, NLAT)
    sines = jnp.sin(math.pi / NLAT * (jnp.arange(NLAT, dtype=jnp.float32) + 0.5))
    weighted = weighted * (sines * math.sqrt(2.0 / NLAT))[None, :]
    north = weighted[:, :half_lat]
    south = jnp.flip(weighted[:, half_lat:], axis=1)
    folded = jnp.pad(
        jnp.stack([north + south, north - south]),
        ((0, 0), (0, round_up(used, 128) - used), (0, lat_padded - half_lat)),
    )
    summed = contract_table(table_high, table_low, *split_pair(folded), columns_per_slot)
    result = summed.transpose(2, 1, 0).reshape(-1, M)[:used]
    inside = jnp.arange(M, dtype=jnp.int32)[None, :] < M - my_waves[:, None]
    result = jnp.where(
        inside[:, None, None, :], result.reshape(slots_own, levels, 2, M), 0.0
    ).transpose(1, 0, 2, 3)
    result = lax.all_to_all(
        result.reshape(groups, own_levels * slots_own * 2, M),
        GROUP,
        split_axis=0,
        concat_axis=0,
        tiled=True,
    )
    result = result.reshape(groups, own_levels, slots_own, 2, M).transpose(1, 0, 2, 3, 4)
    return result.reshape(own_levels, groups * slots_own, 2, M)[:, :slots_lat]


def solution(mesh):
    return jax.shard_map(
        shards,
        mesh=mesh,
        in_specs=(
            P("member", "lat", ("lev", "fld")),
            P("member", "lat", ("lev", "fld")),
            P("member", "lat", ("lev", "fld")),
            P("lat"),
            P(),
        ),
        out_specs=P(("member", "lev", "fld"), "lat", None, None),
        check_vma=False,
    )
```

time: 816 us -> 145 us (0.18)
  local copies, waits for them, and re-layouts: 419 us -> 45.2 us
  matrix products: 211 us -> 4.56 us
  other arithmetic: 129 us -> 24.2 us
  Pallas kernels: 0 us -> 35 us
  waiting for transfers between devices: 35.3 us -> 8.57 us
  blocking collectives: 0 us -> 11.1 us
    dynamic_update_slice x25 -> x0, local copies, waits for them, and re-layouts: 408 us -> none  [advance(): lax.dynamic_update_slice_in_dim(result_now, partial_value, first_order, 3)]
    dot_general x26 -> x1, matrix products: 211 us -> 4.56 us  [shards(): jnp.einsum('sck,ijk->scij', fourier_table(waves, NLON), advected, precisi...]
    while x375 -> x0, other arithmetic: 72.1 us -> none
    pallas_call x0 -> x2, Pallas kernels: none -> 35 us  [the longest x1 17.8 us: legendre_table(): pl.pallas_call(table_kernel, grid=(slots // slot_tile,), in_specs=[coef_s...]
    all_to_all x2, waiting for transfers between devices: 28.7 us -> 8.56 us  [the longest x1 8.24 us: shards(): lax.all_to_all(advected, GROUP, split_axis=0, concat_axis=2, tiled=True)]
    mul x29 -> x5, other arithmetic: 18 us -> 0.13 us  [the longest x2 0.1 us: shards(): weighted = weighted * (sines * math.sqrt(2.0 / NLAT))[None, :]]
    slice x1 -> x6, local copies, waits for them, and re-layouts: 0.79 us -> 18.3 us  [the longest x1 11.7 us: shards(): result = summed.transpose(2, 1, 0).reshape(-1, M)[:used]]
    reshape x1 -> x5, local copies, waits for them, and re-layouts: 3.16 us -> 16.6 us  [the longest x1 14 us: shards(): result.reshape(slots_own, levels, 2, M)]
  transfers between devices with their start and end apart: 6 -> 6, of which waited for: 5 -> 2; matrix products, arithmetic and copies ran while one was open for 2% -> 16% of each run, Pallas kernels for 0% -> 12%
where the time goes in v1:
time: 145 us; the launch traced here: 144 us
  local copies, waits for them, and re-layouts  45.2 us (31%)
  Pallas kernels  35 us (24%)
  other arithmetic  24.2 us (17%)
  starting transfers between devices  15.3 us (11%)
  blocking collectives  11.1 us (8%)
  waiting for transfers between devices  8.57 us (6%)
  matrix products  4.56 us (3%)
    pallas_call x1, Pallas kernels, legendre_table(): pl.pallas_call(table_kernel, grid=(slots // slot_tile,), in_specs=[coef_s...  17.8 us
    pallas_call x1, Pallas kernels, contract_table(): pl.pallas_call(lambda *refs: contract_kernel(columns_per_slot, *refs), gr...  17.2 us
    reshape x1, local copies, waits for them, and re-layouts, shards(): result.reshape(slots_own, levels, 2, M)  14 us
    cos x1, other arithmetic, fourier_table(): return jnp.stack([jnp.cos(angles), -jnp.sin(angles)], axis=1) * factor  12.4 us
    slice x1, local copies, waits for them, and re-layouts, shards(): result = summed.transpose(2, 1, 0).reshape(-1, M)[:used]  11.7 us
    all_to_all x1, blocking collectives, shards(): lax.all_to_all(result.reshape(groups, own_levels * slots_own * 2, M), GRO...  11.1 us
    all_to_all x1, waiting for transfers between devices, shards(): lax.all_to_all(advected, GROUP, split_axis=0, concat_axis=2, tiled=True)  8.24 us
    sub x1, other arithmetic, advect(): centre - 0.5 * east_wind.astype(jnp.float32) * east_diff  4.88 us
  transfers between devices with their start and end apart: 6, of which 2 were waited for; matrix products, arithmetic and copies ran while one was open for 16% of the time, Pallas kernels for 12%

profile of v1, /device:TPU:0, one launch (start us, length us, event | category | flops | bytes accessed | tf_op | source)
XLA Modules:
  0.0 144.2 jit_solution(9416477568558152096)
XLA Ops:
  0.0 0.0 copy-start
  0.0 0.9 fusion.31
  0.9 3.1 %collective-permute-start.3 = (bf16[4,1,400]{2,1,0:T(2,128)(2,1)S(1)}, bf16[4,1,400]{2,1,0:T(2,128)(2,1)S(1)}, u32[]{:S(2)}, u32[]{:S(2)}) collective-permute-start(bf16[4,1,400]{2,1,0:T(2,128)(2,1)S(1)} %get-tuple-element.15), channel_id=1, source_target_pairs={{0,4},{4,8},{8,12},{12,0},{1,5},{5,9},{9,13},{13,1},{2,6},{6,10},{... | collective-permute-start | bytes 9608 | tf_op jit(solution)/shard_map/ppermute | solution.py:27
  4.0 2.1 %collective-permute-start.2 = (bf16[4,1,400]{2,1,0:T(2,128)(2,1)S(1)}, bf16[4,1,400]{2,1,0:T(2,128)(2,1)S(1)}, u32[]{:S(2)}, u32[]{:S(2)}) collective-permute-start(bf16[4,1,400]{2,1,0:T(2,128)(2,1)S(1)} %get-tuple-element.16), channel_id=1, source_target_pairs={{4,0},{8,4},{12,8},{0,12},{5,1},{9,5},{13,9},{1,13},{6,2},{10,6},{... | collective-permute-start | bytes 9608 | tf_op jit(solution)/shard_map/ppermute | solution.py:30
  6.1 1.8 %fusion.33 = (bf16[4,200,1]{2,1,0:T(8,128)(2,1)}, bf16[4,200,1]{2,1,0:T(8,128)(2,1)S(1)}) fusion(bf16[4,200,400]{2,1,0:T(8,128)(2,1)} %param.5), kind=kLoop, calls=%fused_computation.68 | loop fusion | bytes 6400 | tf_op jit(solution)/shard_map/slice | solution.py:28
  7.9 0.0 collective-permute-start.1
  7.9 1.7 %collective-permute-start = (bf16[4,200,1]{2,1,0:T(8,128)(2,1)S(1)}, bf16[4,200,1]{2,1,0:T(8,128)(2,1)}, u32[]{:S(2)}, u32[]{:S(2)}) collective-permute-start(bf16[4,200,1]{2,1,0:T(8,128)(2,1)S(1)} %get-tuple-element.20), channel_id=1, source_target_pairs={{1,0},{2,1},{3,2},{0,3},{5,4},{6,5},{7,6},{4,7},{9,8},{10,9},{11,1... | collective-permute-start | bytes 4808 | tf_op jit(solution)/shard_map/ppermute | solution.py:30
  9.7 0.6 multiply_cosine_fusion.cosine_ref
  10.4 0.0 copy-done
  10.4 1.6 %fusion.32 = (f32[4,199,400]{2,1,0:T(8,128)S(1)}, f32[4,199,400]{2,1,0:T(8,128)}) fusion(bf16[4,200,400]{2,1,0:T(8,128)(2,1)S(1)} %copy-done), kind=kLoop, calls=%fused_computation.67 | loop fusion | bytes 5094400 | tf_op jit(solution)/shard_map/slice | solution.py:55
  12.0 0.0 copy-start.2
  12.0 2.2 %fusion.34 = (f32[4,200,399]{2,1,0:T(8,128)}, f32[4,200,399]{2,1,0:T(8,128)}) fusion(bf16[4,200,400]{2,1,0:T(8,128)(2,1)S(1)} %copy-done), kind=kLoop, calls=%fused_computation.69 | loop fusion | bytes 5107200 | tf_op jit(solution)/shard_map/slice | solution.py:53
  14.2 0.0 copy-start.1
  14.2 0.0 copy-done.2
  14.2 0.1 broadcast_subtract_fusion
  14.3 0.0 collective-permute-done.1
  14.3 1.0 convert_element_type.81
  15.3 0.0 collective-permute-done
  15.3 1.0 convert_element_type.80
  16.2 0.0 collective-permute-done.3
  16.3 0.0 collective-permute-done.2
  16.3 0.0 copy-done.1
  16.3 4.9 %fusion.12 = f32[4,200,400]{2,1,0:T(8,128)} fusion(f32[4,200,1]{2,1,0:T(8,128)S(1)} %convert_element_type.80, f32[4,200,399]{2,1,0:T(8,128)} %get-tuple-element.22, f32[4,200,399]{2,1,0:T(8,128)} %get-tuple-element.21, f32[4,200,1]{2,1,0:T(8,128)S(1)} %convert_element_type.81, f32[4,1,400]{2,1,0:T(1,128)S(1)} %convert_multiply_fusion.1, ...), kind=kLoop, calls=%fused_computation.17 | loop fusion | flops 4800000 | bytes 8320000 | tf_op jit(solution)/shard_map/sub | solution.py:58
  21.2 0.0 copy-start.3
  21.2 4.5 %all-to-all-start = ((f32[4,200,400]{2,1,0:T(8,128)}), f32[4,200,400]{2,1,0:T(8,128)}, u32[]{:S(2)}, u32[]{:S(2)}) async-start(f32[4,200,400]{2,1,0:T(8,128)} %fusion.12), calls=%async_computation | async-start | bytes 3276800 | tf_op jit(solution)/shard_map/all_to_all | solution.py:222
  25.7 0.0 copy-done.3
  25.7 0.1 compare_convert_fusion
  25.9 12.4 %fusion.8 = (f32[400,1,1600]{2,0,1:T(8,128)S(1)}, f32[400,1,1600]{2,0,1:T(8,128)}) fusion(s32[400]{0:T(512)S(1)} %copy-done.2), kind=kLoop, calls=%fused_computation.12 | loop fusion | flops 6400000 | bytes 5121600 | tf_op jit(solution)/shard_map/cos | solution.py:39
  38.3 8.2 %all-to-all-done = f32[4,200,400]{2,1,0:T(8,128)} async-done(((f32[4,200,400]{2,1,0:T(8,128)}), f32[4,200,400]{2,1,0:T(8,128)}, u32[]{:S(2)}, u32[]{:S(2)}) %all-to-all-start) | async-done | bytes 1280032 | tf_op jit(solution)/shard_map/all_to_all | solution.py:222
  46.5 3.7 %copy.29 = f32[1,200,4,400]{3,2,1,0:T(4,128)} copy(f32[1,200,4,400]{3,1,2,0:T(8,128)} %bitcast.1) | data formatting | bytes 2560000 | tf_op jit(solution)/shard_map/all_to_all | solution.py:222
  50.2 3.2 %reshape.236 = f32[200,1600,1]{1,0,2:T(8,128)} reshape(f32[1,200,4,400]{3,2,1,0:T(4,128)} %copy.29) | data formatting | bytes 2560000 | tf_op jit(solution)/shard_map/reshape.1
  53.4 4.6 %fusion.14 = f32[400,2,200]{2,0,1:T(8,128)S(1)} fusion(f32[200,1600,1]{1,0,2:T(8,128)} %reshape.236, f32[400,1,1600]{2,0,1:T(8,128)} %get-tuple-element.26, f32[400,1,1600]{2,0,1:T(8,128)S(1)} %get-tuple-element.25, f32[400,200]{1,0:T(8,128)S(1)} %compare_convert_fusion), kind=kOutput, calls=%fused_computation.22 | convolution fusion | flops 1538720000 | bytes 7360000 | tf_op jit(solution)/shard_map/sck,ijk->scij/dot_general | solution.py:223
  57.9 0.6 copy.30
  58.6 1.5 %reshape.231 = f32[16,50,200]{2,1,0:T(8,128)} reshape(f32[400,2,200]{2,1,0:T(2,128)S(1)} %copy.30) | data formatting | bytes 1280000 | tf_op jit(solution)/shard_map/reshape | solution.py:228
  60.1 3.8 %all-to-all-start.1 = ((f32[16,50,200]{2,1,0:T(8,128)}), f32[16,50,200]{2,1,0:T(8,128)S(1)}, u32[]{:S(2)}, u32[]{:S(2)}) async-start(f32[16,50,200]{2,1,0:T(8,128)} %reshape.231), calls=%async_computation.1 | async-start | bytes 1835008 | tf_op jit(solution)/shard_map/all_to_all | solution.py:229
  63.9 0.2 select_reduce_fusion
  64.1 0.7 multiply_add_fusion.start_ref
  64.8 1.4 fusion.21
  66.2 17.8 %legendre_table.1 = (bf16[2,200,32,512]{3,2,1,0:T(8,128)(2,1)}, bf16[2,200,32,512]{3,2,1,0:T(8,128)(2,1)}) custom-call(f32[25,32,16]{2,1,0:T(8,128)} %get-tuple-element.24.growth_ref, f32[25,32,16]{2,1,0:T(8,128)} %get-tuple-element.23.damping_ref, f32[1,512]{1,0:T(1,128)} %multiply_cosine_fusion.cosine_ref, f32[32,512]{1,0:T(8,128)} %multiply_add_fusion.start_ref), custom_call_target="tpu_custom_call" | custom-call | flops 65536000 | bytes 26214400 | tf_op jit(solution)/shard_map/legendre_table/pallas_call | solution.py:130
  84.0 0.1 iota_compare_fusion.2
  84.1 0.3 all-to-all-done.1
  84.4 0.5 reshape.238
  84.9 0.3 copy.40
  85.3 0.5 reshape.233
  85.8 0.1 broadcast_multiply_fusion
  85.8 0.2 slice.50
  86.0 1.3 reverse
  87.3 0.2 add_bitcast_fusion
  87.5 1.1 fusion.15
  88.7 17.2 %legendre_contract.1 = f32[2,200,256]{2,1,0:T(8,128)} custom-call(bf16[2,200,32,512]{3,2,1,0:T(8,128)(2,1)} %get-tuple-element.7.refs_0_, bf16[2,200,32,512]{3,2,1,0:T(8,128)(2,1)} %get-tuple-element.8.refs_1_, bf16[2,256,512]{2,1,0:T(8,128)(2,1)} %get-tuple-element.14.refs_2_, bf16[2,256,512]{2,1,0:T(8,128)(2,1)} %get-tuple-element.13.refs_3_), custom_call_target="tpu_custom_call" | custom-call | flops 10066329600 | bytes 26214400 | tf_op jit(solution)/shard_map/legendre_contract/pallas_call | solution.py:176
  105.9 11.7 %copy.33 = f32[200,200,2]{2,1,0:T(8,128)} copy(f32[200,200,2]{0,1,2:T(8,128)} %bitcast.23) | data formatting | bytes 640000 | tf_op jit(solution)/shard_map/slice | solution.py:245
  117.5 14.0 %reshape.234 = f32[25,4,2,400]{3,2,1,0:T(2,128)S(1)} reshape(f32[200,200,2]{2,1,0:T(8,128)} %copy.33) | data formatting | bytes 640000 | tf_op jit(solution)/shard_map/reshape | solution.py:248
  131.6 0.2 select_bitcast_fusion
  131.8 0.1 copy.34
  131.9 0.1 copy.35
  132.1 11.1 %all_to_all.25 = f32[4,50,400]{2,1,0:T(8,128)S(1)} all-to-all(f32[4,50,400]{2,1,0:T(8,128)S(1)} %copy.35), channel_id=1, replica_groups=mesh['member'=2,'lat'=4,'lev'=2,'fld'=2] {'lev','fld'}, dimensions={0} | all-to-all | bytes 640000 | tf_op jit(solution)/shard_map/all_to_all | solution.py:250
  143.2 1.0 reshape_transpose_reshape.3
  (10 shorter events, 0.2 us)
Async XLA Ops:
  0.0 10.4 %copy-start = (bf16[4,200,400]{2,1,0:T(8,128)(2,1)S(1)}, bf16[4,200,400]{2,1,0:T(8,128)(2,1)}, u32[]{:S(2)}) copy-start(bf16[4,200,400]{2,1,0:T(8,128)(2,1)} %param.5) | copy-start | bytes 1920004
  0.9 15.4 %collective-permute-start.3 = (bf16[4,1,400]{2,1,0:T(2,128)(2,1)S(1)}, bf16[4,1,400]{2,1,0:T(2,128)(2,1)S(1)}, u32[]{:S(2)}, u32[]{:S(2)}) collective-permute-start(bf16[4,1,400]{2,1,0:T(2,128)(2,1)S(1)} %get-tuple-element.15), channel_id=1, source_target_pairs={{0,4},{4,8},{8,12},{12,0},{1,5},{5,9},{9,13},{13,1},{2,6},{6,10},{... | collective-permute-start | bytes 9608 | tf_op jit(solution)/shard_map/ppermute | solution.py:27
  4.0 12.3 %collective-permute-start.2 = (bf16[4,1,400]{2,1,0:T(2,128)(2,1)S(1)}, bf16[4,1,400]{2,1,0:T(2,128)(2,1)S(1)}, u32[]{:S(2)}, u32[]{:S(2)}) collective-permute-start(bf16[4,1,400]{2,1,0:T(2,128)(2,1)S(1)} %get-tuple-element.16), channel_id=1, source_target_pairs={{4,0},{8,4},{12,8},{0,12},{5,1},{9,5},{13,9},{1,13},{6,2},{10,6},{... | collective-permute-start | bytes 9608 | tf_op jit(solution)/shard_map/ppermute | solution.py:30
  7.9 6.3 %collective-permute-start.1 = (bf16[4,200,1]{2,1,0:T(8,128)(2,1)}, bf16[4,200,1]{2,1,0:T(8,128)(2,1)}, u32[]{:S(2)}, u32[]{:S(2)}) collective-permute-start(bf16[4,200,1]{2,1,0:T(8,128)(2,1)} %get-tuple-element.19), channel_id=1, source_target_pairs={{0,1},{1,2},{2,3},{3,0},{4,5},{5,6},{6,7},{7,4},{8,9},{9,10},{10,1... | collective-permute-start | bytes 4808 | tf_op jit(solution)/shard_map/ppermute | solution.py:27
  7.9 7.4 %collective-permute-start = (bf16[4,200,1]{2,1,0:T(8,128)(2,1)S(1)}, bf16[4,200,1]{2,1,0:T(8,128)(2,1)}, u32[]{:S(2)}, u32[]{:S(2)}) collective-permute-start(bf16[4,200,1]{2,1,0:T(8,128)(2,1)S(1)} %get-tuple-element.20), channel_id=1, source_target_pairs={{1,0},{2,1},{3,2},{0,3},{5,4},{6,5},{7,6},{4,7},{9,8},{10,9},{11,1... | collective-permute-start | bytes 4808 | tf_op jit(solution)/shard_map/ppermute | solution.py:30
  12.0 2.2 %copy-start.2 = (s32[400]{0:T(512)S(1)}, s32[400]{0:T(512)}, u32[]{:S(2)}) copy-start(s32[400]{0:T(512)} %param.9) | copy-start | bytes 4804
  14.2 2.1 %copy-start.1 = (bf16[4,200,400]{2,1,0:T(8,128)(2,1)S(1)}, bf16[4,200,400]{2,1,0:T(8,128)(2,1)}, u32[]{:S(2)}) copy-start(bf16[4,200,400]{2,1,0:T(8,128)(2,1)} %param.7) | copy-start | bytes 1920004
  21.2 4.5 %copy-start.3 = (s32[200]{0:T(256)S(1)}, s32[200]{0:T(256)}, u32[]{:S(2)}) copy-start(s32[200]{0:T(256)} %param.8) | copy-start | bytes 2404
  21.2 25.3 %all-to-all-start = ((f32[4,200,400]{2,1,0:T(8,128)}), f32[4,200,400]{2,1,0:T(8,128)}, u32[]{:S(2)}, u32[]{:S(2)}) async-start(f32[4,200,400]{2,1,0:T(8,128)} %fusion.12), calls=%async_computation | async-start | bytes 3276800 | tf_op jit(solution)/shard_map/all_to_all | solution.py:222
  60.1 24.4 %all-to-all-start.1 = ((f32[16,50,200]{2,1,0:T(8,128)}), f32[16,50,200]{2,1,0:T(8,128)S(1)}, u32[]{:S(2)}, u32[]{:S(2)}) async-start(f32[16,50,200]{2,1,0:T(8,128)} %reshape.231), calls=%async_computation.1 | async-start | bytes 1835008 | tf_op jit(solution)/shard_map/all_to_all | solution.py:229

commit v2 on v1

--- a/solution.py
+++ b/solution.py
@@ -31,34 +31,128 @@
     return low, high
 
 
-def fourier_table(wave_ids, lon_count):
+def fourier_table(row_waves, lon_count, quarter_turns):
     grid_index = jnp.arange(lon_count, dtype=jnp.int32)
-    phase_index = wave_ids[:, None] * grid_index[None, :] % lon_count
+    shift = quarter_turns * (lon_count // 4)
+    phase_index = (row_waves[:, None] * grid_index[None, :] + shift[:, None]) % lon_count
     angles = 2.0 * math.pi / lon_count * phase_index.astype(jnp.float32)
-    factor = 1.0 / math.sqrt(lon_count)
-    return jnp.stack([jnp.cos(angles), -jnp.sin(angles)], axis=1) * factor
+    return jnp.cos(angles) * (1.0 / math.sqrt(lon_count))
+
+
+def advect_kernel(
+    tracer_ref, east_wind_ref, north_wind_ref, west_ref, east_ref, above_ref, below_ref, out_ref, pad_ref
+):
+    _, rows, columns = out_ref.shape
+    tall, wide = pad_ref.shape
+    centre = tracer_ref[0].astype(jnp.float32)
+    pad_ref[:rows, :columns] = centre
+    pad_ref[:rows, columns : columns + 1] = east_ref[0].astype(jnp.float32)
+    pad_ref[:rows, wide - 1 : wide] = west_ref[0].astype(jnp.float32)
+    pad_ref[rows : rows + 1, :columns] = below_ref[0]
+    pad_ref[tall - 1 : tall, :columns] = above_ref[0]
+    full = pad_ref[...]
+    east_diff = (pltpu.roll(full, wide - 1, 1) - pltpu.roll(full, 1, 1))[:rows, :columns]
+    north_diff = (pltpu.roll(full, tall - 1, 0) - pltpu.roll(full, 1, 0))[:rows, :columns]
+    out_ref[0] = (
+        centre
+        - 0.5 * east_wind_ref[0].astype(jnp.float32) * east_diff
+        - 0.5 * north_wind_ref[0].astype(jnp.float32) * north_diff
+    )
 
 
 def advect(tracer, east_wind, north_wind, first_row, lat_total):
     west, east = edges(tracer, GROUP, 2)
     above, below = edges(tracer, "lat", 1)
-    centre = tracer.astype(jnp.float32)
-    rows_here = tracer.shape[1]
+    levels, rows, columns = tracer.shape
     has_above = (first_row > 0).astype(jnp.float32)
-    has_below = (first_row + rows_here < lat_total).astype(jnp.float32)
+    has_below = (first_row + rows < lat_total).astype(jnp.float32)
     above = above.astype(jnp.float32) * has_above
     below = below.astype(jnp.float32) * has_below
-    east_diff = jnp.concatenate(
-        [centre[:, :, 1:], east.astype(jnp.float32)], axis=2
-    ) - jnp.concatenate([west.astype(jnp.float32), centre[:, :, :-1]], axis=2)
-    north_diff = jnp.concatenate([centre[:, 1:], below], axis=1) - jnp.concatenate(
-        [above, centre[:, :-1]], axis=1
-    )
-    return (
-        centre
-        - 0.5 * east_wind.astype(jnp.float32) * east_diff
-        - 0.5 * north_wind.astype(jnp.float32) * north_diff
-    )
+    block = pl.BlockSpec((1, rows, columns), lambda i: (i, 0, 0))
+    column = pl.BlockSpec((1, rows, 1), lambda i: (i, 0, 0))
+    line = pl.BlockSpec((1, 1, columns), lambda i: (i, 0, 0))
+    size = levels * rows * columns
+    return pl.pallas_call(
+        advect_kernel,
+        grid=(levels,),
+        in_specs=[block, block, block, column, column, line, line],
+        out_specs=block,
+        out_shape=jax.ShapeDtypeStruct(tracer.shape, jnp.float32),
+        scratch_shapes=[pltpu.VMEM((round_up(rows + 2, 8), round_up(columns + 2, 128)), jnp.float32)],
+        cost_estimate=pl.CostEstimate(
+            flops=10 * size, bytes_accessed=10 * size, transcendentals=0
+        ),
+        name="advect",
+    )(tracer, east_wind, north_wind, west, east, above, below)
+
+
+def split_high_low(values):
+    high = values.astype(jnp.bfloat16)
+    return high, (values - high.astype(jnp.float32)).astype(jnp.bfloat16)
+
+
+def product(left, right):
+    return lax.dot_general(
+        left, right, (((1,), (1,)), ((), ())), preferred_element_type=jnp.float32
+    )
+
+
+def fourier_kernel(rows_own, table_ref, field_ref, wave_ref, keep_ref, out_ref, total_ref):
+    step = pl.program_id(0)
+    _, levels, lat_rows, _ = field_ref.shape
+    targets = out_ref.shape[0]
+    rows_padded = table_ref.shape[1] // targets
+    table_high, table_low = split_high_low(table_ref[0])
+    for level in range(levels):
+        field_high, field_low = split_high_low(field_ref[0, level])
+        term = (
+            product(table_high, field_high)
+            + product(table_high, field_low)
+            + product(table_low, field_high)
+        )
+
+        @pl.when(step == 0)
+        def _():
+            total_ref[level] = term
+
+        @pl.when(step > 0)
+        def _():
+            total_ref[level] += term
+
+    @pl.when(step == pl.num_programs(0) - 1)
+    def _():
+        kept = wave_ref[...] < keep_ref[...]
+        for level in range(levels):
+            masked = jnp.where(kept, total_ref[level], 0.0)
+            for target in range(targets):
+                first = target * rows_padded
+                out_ref[target, level * rows_own : (level + 1) * rows_own] = masked[
+                    first : first + rows_own
+                ]
+
+
+def fourier_transform(table, field, row_waves, keep_m, targets, rows_own):
+    chunks, levels, lat_rows, lons = field.shape
+    rows = row_waves.shape[0]
+    return pl.pallas_call(
+        lambda *refs: fourier_kernel(rows_own, *refs),
+        grid=(chunks,),
+        in_specs=[
+            pl.BlockSpec((1, rows, lons), lambda i: (i, 0, 0)),
+            pl.BlockSpec((1, levels, lat_rows, lons), lambda i: (i, 0, 0, 0)),
+            pl.BlockSpec((rows, 1), lambda i: (0, 0)),
+            pl.BlockSpec((1, lat_rows), lambda i: (0, 0)),
+        ],
+        out_specs=pl.BlockSpec((targets, levels * rows_own, lat_rows), lambda i: (0, 0, 0)),
+        out_shape=jax.ShapeDtypeStruct((targets, levels * rows_own, lat_rows), jnp.float32),
+        scratch_shapes=[pltpu.VMEM((levels, rows, lat_rows), jnp.float32)],
+        cost_estimate=pl.CostEstimate(
+            flops=6 * rows * chunks * levels * lat_rows * lons,
+            bytes_accessed=4 * rows * chunks * lons,
+            transcendentals=0,
+        ),
+        name="fourier_transform",
+    )(table, field, row_waves[:, None], keep_m[None, :])
 
 
 def legendre_setup(wave_ids, trunc_count, lat_total, lat_used, lat_padded):
@@ -145,47 +239,66 @@
     )(growth, damping, cosine, start_log)
 
 
-def contract_kernel(columns_per_slot, high_ref, low_ref, weight_high_ref, weight_low_ref, out_ref):
+def contract_kernel(
+    high_ref, low_ref, weight_high_ref, weight_low_ref, own_ref, limit_ref, out_ref, sums_ref
+):
+    step = pl.program_id(0)
     _, orders, slots, lats = high_ref.shape
-    columns = out_ref.shape[2]
-    high = high_ref[0].reshape(orders * slots, lats)
-    low = low_ref[0].reshape(orders * slots, lats)
-
-    def dot(left, right):
-        return lax.dot_general(
-            left, right, (((1,), (1,)), ((), ())), preferred_element_type=jnp.float32
+    lane_tiles, _, lanes = sums_ref.shape
+    levels, rows_own, order_total = out_ref.shape
+    own = own_ref[...] > 0.0
+    for parity in range(2):
+        high = high_ref[parity].reshape(orders * slots, lats)
+        low = low_ref[parity].reshape(orders * slots, lats)
+        full = (
+            product(high, weight_high_ref[parity])
+            + product(high, weight_low_ref[parity])
+            + product(low, weight_high_ref[parity])
         )
-
-    full = (
-        dot(high, weight_high_ref[0]) + dot(high, weight_low_ref[0]) + dot(low, weight_high_ref[0])
-    )
-    slot_of_row = lax.broadcasted_iota(jnp.int32, (slots, columns), 0)
-    column = lax.broadcasted_iota(jnp.int32, (slots, columns), 1)
-    first = slot_of_row * columns_per_slot
-    own = (column >= first) & (column < first + columns_per_slot)
-    picked = jnp.where(own[None], full.reshape(orders, slots, columns), 0.0)
-    out_ref[0] = jnp.sum(picked, axis=1)
-
-
-def contract_table(high, low, weight_high, weight_low, columns_per_slot):
+        picked = jnp.where(own[None], full.reshape(orders, slots, lane_tiles * lanes), 0.0)
+        summed = jnp.sum(picked, axis=1)
+        for tile in range(lane_tiles):
+            sums_ref[tile, pl.ds(step * 2 * orders + parity, orders, stride=2), :] = summed[
+                :, tile * lanes : (tile + 1) * lanes
+            ]
+
+    @pl.when(step == pl.num_programs(0) - 1)
+    def _():
+        turned = jnp.concatenate([sums_ref[tile].T for tile in range(lane_tiles)], axis=0)
+        turned = turned[:, :order_total]
+        order = lax.broadcasted_iota(jnp.int32, turned.shape, 1)
+        turned = jnp.where(order < limit_ref[...], turned, 0.0)
+        for level in range(levels):
+            out_ref[level] = turned[level * rows_own : (level + 1) * rows_own]
+
+
+def contract_table(high, low, weight_high, weight_low, own, limit, levels, rows_own):
     _, half, slots, lats = high.shape
     columns = weight_high.shape[1]
-    tile = 40
-    table_spec = pl.BlockSpec((1, tile, slots, lats), lambda p, i: (p, i, 0, 0))
-    weight_spec = pl.BlockSpec((1, columns, lats), lambda p, i: (p, 0, 0))
+    tile = 20
+    table_spec = pl.BlockSpec((2, tile, slots, lats), lambda i: (0, i, 0, 0))
+    weight_spec = pl.BlockSpec((2, columns, lats), lambda i: (0, 0, 0))
     return pl.pallas_call(
-        lambda *refs: contract_kernel(columns_per_slot, *refs),
-        grid=(2, half // tile),
-        in_specs=[table_spec, table_spec, weight_spec, weight_spec],
-        out_specs=pl.BlockSpec((1, tile, columns), lambda p, i: (p, i, 0)),
-        out_shape=jax.ShapeDtypeStruct((2, half, columns), jnp.float32),
+        contract_kernel,
+        grid=(half // tile,),
+        in_specs=[
+            table_spec,
+            table_spec,
+            weight_spec,
+            weight_spec,
+            pl.BlockSpec((slots, columns), lambda i: (0, 0)),
+            pl.BlockSpec((columns, 1), lambda i: (0, 0)),
+        ],
+        out_specs=pl.BlockSpec((levels, rows_own, 2 * half), lambda i: (0, 0, 0)),
+        out_shape=jax.ShapeDtypeStruct((levels, rows_own, 2 * half), jnp.float32),
+        scratch_shapes=[pltpu.VMEM((columns // 128, round_up(2 * half, 128), 128), jnp.float32)],
         cost_estimate=pl.CostEstimate(
             flops=12 * half * slots * lats * columns,
             bytes_accessed=8 * half * slots * lats,
             transcendentals=0,
         ),
         name="legendre_contract",
-    )(high, low, weight_high, weight_low)
+    )(high, low, weight_high, weight_low, own, limit)
 
 
 def split_pair(values):
@@ -218,42 +331,45 @@
         *legendre_setup(padded_waves, M, NLAT, half_lat, lat_padded)
     )
 
+    targets = lat_parts * groups
+    rows_own = slots_own * 2
+    rows_padded = round_up(rows_own, 8)
+    row_waves = jnp.pad(
+        jnp.repeat(waves.reshape(targets, slots_own), 2, axis=1),
+        ((0, 0), (0, rows_padded - rows_own)),
+        constant_values=M,
+    ).reshape(-1)
+    table = fourier_table(row_waves, NLON, jnp.arange(targets * rows_padded, dtype=jnp.int32) % 2)
+    table = table.reshape(-1, groups, NLON // groups).transpose(1, 0, 2)
+
     advected = advect(tracer, wind_east, wind_north, first_row, NLAT)
-    advected = lax.all_to_all(advected, GROUP, split_axis=0, concat_axis=2, tiled=True)
-    fourier = jnp.einsum(
-        "sck,ijk->scij", fourier_table(waves, NLON), advected, precision=lax.Precision.HIGH
-    )
-    kept_mask = (waves[:, None] < keep_m[None, :]).astype(jnp.float32)
-    fourier = fourier * kept_mask[:, None, None, :]
-    fourier = fourier.reshape(lat_parts * groups, slots_own * 2 * own_levels, lat_rows)
+    advected = lax.all_to_all(advected, GROUP, split_axis=0, concat_axis=0, tiled=True)
+    advected = advected.reshape(groups, own_levels, lat_rows, -1)
+    fourier = fourier_transform(table, advected, row_waves, keep_m, targets, rows_own)
     spectral_in = lax.all_to_all(
         fourier, ("lat",) + GROUP, split_axis=0, concat_axis=0, tiled=True
     )
-    spectral_in = spectral_in.reshape(lat_parts, groups, slots_own, 2, own_levels, lat_rows)
-    columns_per_slot = levels * 2
-    used = slots_own * columns_per_slot
-    weighted = spectral_in.transpose(2, 1, 4, 3, 0, 5).reshape(used, NLAT)
+    used = levels * rows_own
+    weighted = spectral_in.reshape(lat_parts, used, lat_rows).transpose(1, 0, 2)
+    weighted = weighted.reshape(used, NLAT)
     sines = jnp.sin(math.pi / NLAT * (jnp.arange(NLAT, dtype=jnp.float32) + 0.5))
     weighted = weighted * (sines * math.sqrt(2.0 / NLAT))[None, :]
     north = weighted[:, :half_lat]
     south = jnp.flip(weighted[:, half_lat:], axis=1)
+    columns = round_up(used, 128)
     folded = jnp.pad(
         jnp.stack([north + south, north - south]),
-        ((0, 0), (0, round_up(used, 128) - used), (0, lat_padded - half_lat)),
-    )
-    summed = contract_table(table_high, table_low, *split_pair(folded), columns_per_slot)
-    result = summed.transpose(2, 1, 0).reshape(-1, M)[:used]
-    inside = jnp.arange(M, dtype=jnp.int32)[None, :] < M - my_waves[:, None]
-    result = jnp.where(
-        inside[:, None, None, :], result.reshape(slots_own, levels, 2, M), 0.0
-    ).transpose(1, 0, 2, 3)
-    result = lax.all_to_all(
-        result.reshape(groups, own_levels * slots_own * 2, M),
-        GROUP,
-        split_axis=0,
-        concat_axis=0,
-        tiled=True,
-    )
+        ((0, 0), (0, columns - used), (0, lat_padded - half_lat)),
+    )
+    slot_of_column = jnp.arange(columns, dtype=jnp.int32) % rows_own // 2
+    own = (jnp.arange(slots_padded, dtype=jnp.int32)[:, None] == slot_of_column[None, :]).astype(
+        jnp.float32
+    )
+    limit = (M - my_waves)[slot_of_column][:, None]
+    result = contract_table(
+        table_high, table_low, *split_pair(folded), own, limit, levels, rows_own
+    )
+    result = lax.all_to_all(result, GROUP, split_axis=0, concat_axis=0, tiled=True)
     result = result.reshape(groups, own_levels, slots_own, 2, M).transpose(1, 0, 2, 3, 4)
     return result.reshape(own_levels, groups * slots_own, 2, M)[:, :slots_lat]
 

time: 145 us -> 142 us (0.979)
  local copies, waits for them, and re-layouts: 45.2 us -> 12.1 us
  other arithmetic: 24.2 us -> 53.8 us
  Pallas kernels: 35 us -> 47.8 us
  waiting for transfers between devices: 8.57 us -> 0.02 us
  matrix products: 4.56 us -> 0 us
    mul x0 -> x3, other arithmetic: none -> 30.2 us  [the longest x1 30.2 us: fourier_table(): return jnp.cos(angles) * (1.0 / math.sqrt(lon_count))]
    gather x0 -> x20, other arithmetic: none -> 16.5 us  [shards(): limit = (M - my_waves)[slot_of_column][:, None]]
    slice x5 -> x2, local copies, waits for them, and re-layouts: 18.2 us -> 1.95 us  [edges(): high = lax.ppermute(lax.slice_in_dim(block, 0, 1, axis=dim), axis, backward)]
    reshape x5 -> x3, local copies, waits for them, and re-layouts: 16.6 us -> 0.62 us  [the longest x1 0.5 us: shards(): weighted = weighted.reshape(used, NLAT)]
    pallas_call x1 -> x3, Pallas kernels: 17.2 us -> 29.9 us  [the longest x1 17.8 us: contract_table(): pl.pallas_call(contract_kernel, grid=(half // tile,), in_specs=[table_spe...]
    cos x1 -> x0, other arithmetic: 12.4 us -> none  [fourier_table(): return jnp.stack([jnp.cos(angles), -jnp.sin(angles)], axis=1) * factor]
    all_to_all x1, waiting for transfers between devices: 8.24 us -> 0.01 us  [shards(): lax.all_to_all(advected, GROUP, split_axis=0, concat_axis=0, tiled=True)]
    dot_general x1 -> x0, matrix products: 4.56 us -> none  [shards(): jnp.einsum('sck,ijk->scij', fourier_table(waves, NLON), advected, precisi...]
  transfers between devices with their start and end apart: 6 -> 6, of which waited for: 2 -> 0; matrix products, arithmetic and copies ran while one was open for 16% -> 41% of each run, Pallas kernels for 12% -> 13%
where the time goes in v2:
time: 142 us; the launch traced here: 141 us
  other arithmetic  53.8 us (38%)
  Pallas kernels  47.8 us (34%)
  starting transfers between devices  15.9 us (11%)
  local copies, waits for them, and re-layouts  12.1 us (9%)
  blocking collectives  11.5 us (8%)
    mul x1, other arithmetic, fourier_table(): return jnp.cos(angles) * (1.0 / math.sqrt(lon_count))  30.2 us
    pallas_call x1, Pallas kernels, legendre_table(): pl.pallas_call(table_kernel, grid=(slots // slot_tile,), in_specs=[coef_s...  17.9 us
    pallas_call x1, Pallas kernels, contract_table(): pl.pallas_call(contract_kernel, grid=(half // tile,), in_specs=[table_spe...  17.8 us
    gather x20, other arithmetic, shards(): limit = (M - my_waves)[slot_of_column][:, None]  16.5 us
    all_to_all x1, blocking collectives, shards(): lax.all_to_all(result, GROUP, split_axis=0, concat_axis=0, tiled=True)  11.5 us
    pallas_call x1, Pallas kernels, fourier_transform(): pl.pallas_call(lambda *refs: fourier_kernel(rows_own, *refs), grid=(chunk...  7.49 us
    all_to_all x1, starting transfers between devices, shards(): lax.all_to_all(fourier, ('lat',) + GROUP, split_axis=0, concat_axis=0, ti...  6.48 us
    ppermute x2, starting transfers between devices, edges(): high = lax.ppermute(lax.slice_in_dim(block, 0, 1, axis=dim), axis, backward)  5.83 us
  transfers between devices with their start and end apart: 6, of which 0 were waited for; matrix products, arithmetic and copies ran while one was open for 41% of the time, Pallas kernels for 13%

profile of v2, /device:TPU:0, one launch (start us, length us, event | category | flops | bytes accessed | tf_op | source)
XLA Modules:
  0.0 141.3 jit_solution(3072329834514733987)
XLA Ops:
  0.0 0.8 fusion.26
  0.8 5.1 %collective-permute-start.3 = (bf16[4,1,400]{2,1,0:T(2,128)(2,1)S(1)}, bf16[4,1,400]{2,1,0:T(2,128)(2,1)S(1)}, u32[]{:S(2)}, u32[]{:S(2)}) collective-permute-start(bf16[4,1,400]{2,1,0:T(2,128)(2,1)S(1)} %get-tuple-element.15), channel_id=1, source_target_pairs={{4,0},{8,4},{12,8},{0,12},{5,1},{9,5},{13,9},{1,13},{6,2},{10,6},{... | collective-permute-start | bytes 9608 | tf_op jit(solution)/shard_map/ppermute | solution.py:30
  5.9 0.0 collective-permute-start.2
  5.9 1.2 fusion.27
  7.1 0.7 collective-permute-start.1
  7.8 0.0 collective-permute-start
  8.5 0.7 multiply_cosine_fusion.cosine_ref
  9.3 0.8 reshape_reshape.3
  10.0 0.8 broadcast_subtract_fusion
  10.8 0.7 fusion.29
  11.5 0.7 fusion.28
  12.2 0.1 copy.24
  12.3 0.1 copy.31
  12.4 0.1 mul.198
  12.5 1.0 broadcast_in_dim_reshape.5.refs_2_
  13.5 0.2 select_reduce_fusion
  13.8 0.0 collective-permute-done.3
  13.8 0.6 convert_multiply_fusion.below_ref
  14.4 0.0 collective-permute-done.2
  14.4 0.6 convert_multiply_fusion.1.above_ref
  15.0 0.0 collective-permute-done.1.east_ref
  15.0 0.0 copy-start.1
  15.0 0.0 collective-permute-done.west_ref
  15.0 0.7 copy-done.1
  15.7 0.0 copy-start.2
  15.7 0.7 copy-done.2
  16.4 4.6 %advect.1 = f32[4,200,400]{2,1,0:T(8,128)} custom-call(bf16[4,200,400]{2,1,0:T(8,128)(2,1)} %tracer_ref.1, bf16[4,200,400]{2,1,0:T(8,128)(2,1)} %east_wind_ref.1, bf16[4,200,400]{2,1,0:T(8,128)(2,1)} %north_wind_ref.1, bf16[4,200,1]{2,1,0:T(8,128)(2,1)} %copy-done.2, bf16[4,200,1]{2,1,0:T(8,128)(2,1)} %copy-done.1, ...), custom_call_target="tpu_custom_call" | custom-call | flops 3200000 | bytes 3200000 | tf_op jit(solution)/shard_map/advect/pallas_call | solution.py:75
  21.0 3.6 %all-to-all-start = ((f32[4,200,400]{2,1,0:T(8,128)}), f32[4,200,400]{2,1,0:T(8,128)S(1)}, u32[]{:S(2)}, u32[]{:S(2)}) async-start(f32[4,200,400]{2,1,0:T(8,128)} %advect.1), calls=%async_computation | async-start | bytes 3276800 | tf_op jit(solution)/shard_map/all_to_all | solution.py:346
  24.6 4.3 %compare_select_fusion.1 = s32[256,1]{0,1:T(1,128)S(1)} fusion(s32[]{:T(128)} %bitcast.23, s32[]{:T(128)} %bitcast.24, s32[]{:T(128)} %bitcast.25, s32[]{:T(128)} %bitcast.26, s32[]{:T(128)} %bitcast.27, s32[]{:T(128)} %bitcast.29, s32[]{:T(128)} %bitcast.28), kind=kLoop, calls=%fused_computation.68 | loop fusion | flops 9216 | bytes 1052 | tf_op jit(solution)/shard_map/gather | solution.py:368
  28.9 11.4 %select_select_fusion = s32[256]{0:T(256)S(1)} fusion(pred[256]{0:T(512)(128)(4,1)S(1)} %compare_reduce_fusion, pred[256]{0:T(512)(128)(4,1)S(1)} %compare_reduce_fusion.1, pred[256]{0:T(512)(128)(4,1)S(1)} %compare_reduce_fusion.2, pred[256]{0:T(512)(128)(4,1)S(1)} %compare_reduce_fusion.3, pred[256]{0:T(512)(128)(4,1)S(1)} %compare_reduce_fusion.4, ...), kind=kLoop, calls=%fused_computation.88 | loop fusion | flops 4608 | bytes 6728 | tf_op jit(solution)/shard_map/gather | solution.py:368
  40.3 30.2 %fusion.3.refs_0_ = f32[4,896,400]{2,1,0:T(8,128)} fusion(s32[896]{0:T(1024)S(1)} %fusion.21, s32[4,400]{1,0:T(4,128)S(1)} %multiply_add_fusion.1, s32[896]{0:T(1024)S(1)} %mul.198), kind=kLoop, calls=%fused_computation.4 | loop fusion | flops 15769600 | bytes 5747968 | tf_op jit(solution)/shard_map/mul | solution.py:39
  70.5 0.0 all-to-all-done
  70.5 0.0 copy-start
  70.5 1.3 copy-done
  71.8 7.5 %fourier_transform.1 = f32[16,50,200]{2,1,0:T(8,128)} custom-call(f32[4,896,400]{2,1,0:T(8,128)} %fusion.3.refs_0_, f32[4,1,200,400]{3,2,1,0:T(8,128)} %bitcast.37, s32[896,1]{1,0:T(8,128)} %broadcast_in_dim_reshape.5.refs_2_, s32[1,200]{1,0:T(1,128)} %bitcast.42), custom_call_target="tpu_custom_call" | custom-call | flops 1720320000 | bytes 5734400 | tf_op jit(solution)/shard_map/fourier_transform/pallas_call | solution.py:137
  79.3 6.5 %all-to-all-start.1 = ((f32[16,50,200]{2,1,0:T(8,128)}), f32[16,50,200]{2,1,0:T(8,128)S(1)}, u32[]{:S(2)}, u32[]{:S(2)}) async-start(f32[16,50,200]{2,1,0:T(8,128)} %fourier_transform.1), calls=%async_computation.1 | async-start | bytes 1835008 | tf_op jit(solution)/shard_map/all_to_all | solution.py:349
  85.8 0.8 copy.29.limit_ref
  86.6 0.7 multiply_add_fusion.start_ref
  87.3 1.4 fusion.13
  88.6 17.9 %legendre_table.1 = (bf16[2,200,32,512]{3,2,1,0:T(8,128)(2,1)}, bf16[2,200,32,512]{3,2,1,0:T(8,128)(2,1)}) custom-call(f32[25,32,16]{2,1,0:T(8,128)} %get-tuple-element.20.growth_ref, f32[25,32,16]{2,1,0:T(8,128)} %get-tuple-element.19.damping_ref, f32[1,512]{1,0:T(1,128)} %multiply_cosine_fusion.cosine_ref, f32[32,512]{1,0:T(8,128)} %multiply_add_fusion.start_ref), custom_call_target="tpu_custom_call" | custom-call | flops 65536000 | bytes 26214400 | tf_op jit(solution)/shard_map/legendre_table/pallas_call | solution.py:224
  106.6 0.6 fusion.20.own_ref
  107.2 0.0 all-to-all-done.1
  107.2 0.1 reshape.229
  107.3 0.3 copy.28
  107.7 0.5 reshape.230
  108.2 0.1 broadcast_multiply_fusion
  108.2 0.2 slice.51
  108.4 1.3 reverse
  109.7 0.2 add_bitcast_fusion
  109.9 1.1 fusion.7
  111.0 17.8 %legendre_contract.1 = f32[4,50,400]{2,1,0:T(8,128)} custom-call(bf16[2,200,32,512]{3,2,1,0:T(8,128)(2,1)} %get-tuple-element.7.high_ref, bf16[2,200,32,512]{3,2,1,0:T(8,128)(2,1)} %get-tuple-element.8.low_ref, bf16[2,256,512]{2,1,0:T(8,128)(2,1)} %get-tuple-element.14.weight_high_ref, bf16[2,256,512]{2,1,0:T(8,128)(2,1)} %get-tuple-element.13.weight_low_ref, ...), custom_call_target="tpu_custom_call" | custom-call | flops 10066329600 | bytes 26214400 | tf_op jit(solution)/shard_map/legendre_contract/pallas_call | solution.py:281
  128.8 11.5 %all_to_all.15 = f32[4,50,400]{2,1,0:T(8,128)S(1)} all-to-all(f32[4,50,400]{2,1,0:T(8,128)} %legendre_contract.1), channel_id=1, replica_groups=mesh['member'=2,'lat'=4,'lev'=2,'fld'=2] {'lev','fld'}, dimensions={0} | all-to-all | bytes 640000 | tf_op jit(solution)/shard_map/all_to_all | solution.py:372
  140.3 1.0 reshape_transpose_reshape.3
  (32 shorter events, 1.0 us)
Async XLA Ops:
  0.8 13.0 %collective-permute-start.3 = (bf16[4,1,400]{2,1,0:T(2,128)(2,1)S(1)}, bf16[4,1,400]{2,1,0:T(2,128)(2,1)S(1)}, u32[]{:S(2)}, u32[]{:S(2)}) collective-permute-start(bf16[4,1,400]{2,1,0:T(2,128)(2,1)S(1)} %get-tuple-element.15), channel_id=1, source_target_pairs={{4,0},{8,4},{12,8},{0,12},{5,1},{9,5},{13,9},{1,13},{6,2},{10,6},{... | collective-permute-start | bytes 9608 | tf_op jit(solution)/shard_map/ppermute | solution.py:30
  5.9 8.5 %collective-permute-start.2 = (bf16[4,1,400]{2,1,0:T(2,128)(2,1)S(1)}, bf16[4,1,400]{2,1,0:T(2,128)(2,1)S(1)}, u32[]{:S(2)}, u32[]{:S(2)}) collective-permute-start(bf16[4,1,400]{2,1,0:T(2,128)(2,1)S(1)} %get-tuple-element.16), channel_id=1, source_target_pairs={{0,4},{4,8},{8,12},{12,0},{1,5},{5,9},{9,13},{13,1},{2,6},{6,10},{... | collective-permute-start | bytes 9608 | tf_op jit(solution)/shard_map/ppermute | solution.py:27
  7.1 7.9 %collective-permute-start.1 = (bf16[4,200,1]{2,1,0:T(8,128)(2,1)S(1)}, bf16[4,200,1]{2,1,0:T(8,128)(2,1)S(1)}, u32[]{:S(2)}, u32[]{:S(2)}) collective-permute-start(bf16[4,200,1]{2,1,0:T(8,128)(2,1)S(1)} %get-tuple-element.17), channel_id=1, source_target_pairs={{1,0},{2,1},{3,2},{0,3},{5,4},{6,5},{7,6},{4,7},{9,8},{10,9},{11,1... | collective-permute-start | bytes 4808 | tf_op jit(solution)/shard_map/ppermute | solution.py:30
  7.8 7.2 %collective-permute-start = (bf16[4,200,1]{2,1,0:T(8,128)(2,1)S(1)}, bf16[4,200,1]{2,1,0:T(8,128)(2,1)S(1)}, u32[]{:S(2)}, u32[]{:S(2)}) collective-permute-start(bf16[4,200,1]{2,1,0:T(8,128)(2,1)S(1)} %get-tuple-element.18), channel_id=1, source_target_pairs={{0,1},{1,2},{2,3},{3,0},{4,5},{5,6},{6,7},{7,4},{8,9},{9,10},{10,1... | collective-permute-start | bytes 4808 | tf_op jit(solution)/shard_map/ppermute | solution.py:27
  15.0 0.7 copy-start.1
  15.7 0.7 copy-start.2
  21.0 49.5 %all-to-all-start = ((f32[4,200,400]{2,1,0:T(8,128)}), f32[4,200,400]{2,1,0:T(8,128)S(1)}, u32[]{:S(2)}, u32[]{:S(2)}) async-start(f32[4,200,400]{2,1,0:T(8,128)} %advect.1), calls=%async_computation | async-start | bytes 3276800 | tf_op jit(solution)/shard_map/all_to_all | solution.py:346
  70.5 1.3 copy-start
  79.3 28.0 %all-to-all-start.1 = ((f32[16,50,200]{2,1,0:T(8,128)}), f32[16,50,200]{2,1,0:T(8,128)S(1)}, u32[]{:S(2)}, u32[]{:S(2)}) async-start(f32[16,50,200]{2,1,0:T(8,128)} %fourier_transform.1), calls=%async_computation.1 | async-start | bytes 1835008 | tf_op jit(solution)/shard_map/all_to_all | solution.py:349

commit v3 on v2

--- a/solution.py
+++ b/solution.py
@@ -12,7 +12,9 @@
 NLON = 1600
 
 block_rows = 16
-slot_tile = 16
+slot_tile = 8
+order_tile = 80
+LANES = 128
 GROUP = ("lev", "fld")
 
 
@@ -31,12 +33,54 @@
     return low, high
 
 
-def fourier_table(row_waves, lon_count, quarter_turns):
-    grid_index = jnp.arange(lon_count, dtype=jnp.int32)
+def fourier_factors(row_waves, quarter_turns, offsets, lon_count):
+    step = 2.0 * math.pi / lon_count
+    lane = row_waves[:, None] * jnp.arange(LANES, dtype=jnp.int32)[None, :] % lon_count
+    lane = step * lane.astype(jnp.float32)
     shift = quarter_turns * (lon_count // 4)
-    phase_index = (row_waves[:, None] * grid_index[None, :] + shift[:, None]) % lon_count
-    angles = 2.0 * math.pi / lon_count * phase_index.astype(jnp.float32)
-    return jnp.cos(angles) * (1.0 / math.sqrt(lon_count))
+    base = (offsets[:, None] * row_waves[None, :] + shift[None, :]) % lon_count
+    base = step * base.astype(jnp.float32)
+    factor = 1.0 / math.sqrt(lon_count)
+    return (jnp.cos(base) * factor).T, (jnp.sin(base) * factor).T, jnp.cos(lane), jnp.sin(lane)
+
+
+def wave_table_kernel(base_cos_ref, base_sin_ref, lane_cos_ref, lane_sin_ref, high_ref, low_ref):
+    chunks, _, wide = high_ref.shape
+    tiles = wide // LANES
+    lane_cos = lane_cos_ref[...]
+    lane_sin = lane_sin_ref[...]
+    for chunk in range(chunks):
+        for tile in range(tiles):
+            k = chunk * tiles + tile
+            values = (
+                base_cos_ref[:, k : k + 1] * lane_cos - base_sin_ref[:, k : k + 1] * lane_sin
+            )
+            high, low = split_high_low(values)
+            high_ref[chunk, :, tile * LANES : (tile + 1) * LANES] = high
+            low_ref[chunk, :, tile * LANES : (tile + 1) * LANES] = low
+
+
+def fourier_table(row_waves, quarter_turns, chunks, lons, lon_count):
+    tiles = -(-lons // LANES)
+    offsets = (
+        jnp.arange(chunks, dtype=jnp.int32)[:, None] * lons
+        + jnp.arange(tiles, dtype=jnp.int32)[None, :] * LANES
+    ).reshape(-1)
+    factors = fourier_factors(row_waves, quarter_turns, offsets, lon_count)
+    rows = row_waves.shape[0]
+    tall = math.gcd(rows, 128)
+    out = jax.ShapeDtypeStruct((chunks, rows, tiles * LANES), jnp.bfloat16)
+    out_spec = pl.BlockSpec((chunks, tall, tiles * LANES), lambda i: (0, i, 0))
+    size = chunks * rows * tiles * LANES
+    return pl.pallas_call(
+        wave_table_kernel,
+        grid=(rows // tall,),
+        in_specs=[pl.BlockSpec((tall, f.shape[1]), lambda i: (i, 0)) for f in factors],
+        out_specs=[out_spec, out_spec],
+        out_shape=[out, out],
+        cost_estimate=pl.CostEstimate(flops=8 * size, bytes_accessed=4 * size, transcendentals=0),
+        name="fourier_table",
+    )(*factors)
 
 
 def advect_kernel(
@@ -97,12 +141,15 @@
     )
 
 
-def fourier_kernel(rows_own, table_ref, field_ref, wave_ref, keep_ref, out_ref, total_ref):
+def fourier_kernel(
+    rows_own, table_high_ref, table_low_ref, field_ref, wave_ref, keep_ref, out_ref, total_ref
+):
     step = pl.program_id(0)
-    _, levels, lat_rows, _ = field_ref.shape
+    _, levels, lat_rows, lons = field_ref.shape
     targets = out_ref.shape[0]
-    rows_padded = table_ref.shape[1] // targets
-    table_high, table_low = split_high_low(table_ref[0])
+    rows_padded = table_high_ref.shape[1] // targets
+    table_high = table_high_ref[0][:, :lons]
+    table_low = table_low_ref[0][:, :lons]
     for level in range(levels):
         field_high, field_low = split_high_low(field_ref[0, level])
         term = (
@@ -134,11 +181,13 @@
 def fourier_transform(table, field, row_waves, keep_m, targets, rows_own):
     chunks, levels, lat_rows, lons = field.shape
     rows = row_waves.shape[0]
+    table_spec = pl.BlockSpec((1, rows, table[0].shape[2]), lambda i: (i, 0, 0))
     return pl.pallas_call(
         lambda *refs: fourier_kernel(rows_own, *refs),
         grid=(chunks,),
         in_specs=[
-            pl.BlockSpec((1, rows, lons), lambda i: (i, 0, 0)),
+            table_spec,
+            table_spec,
             pl.BlockSpec((1, levels, lat_rows, lons), lambda i: (i, 0, 0, 0)),
             pl.BlockSpec((rows, 1), lambda i: (0, 0)),
             pl.BlockSpec((1, lat_rows), lambda i: (0, 0)),
@@ -152,7 +201,7 @@
             transcendentals=0,
         ),
         name="fourier_transform",
-    )(table, field, row_waves[:, None], keep_m[None, :])
+    )(*table, field, row_waves[:, None], keep_m[None, :])
 
 
 def legendre_setup(wave_ids, trunc_count, lat_total, lat_used, lat_padded):
@@ -182,89 +231,115 @@
     return blocked(growth), blocked(damping), jnp.cos(colatitude)[None, :], start_log
 
 
-def table_kernel(growth_ref, damping_ref, cosine_ref, start_ref, high_ref, low_ref):
-    cosine = cosine_ref[...]
+def table_kernel(
+    blocks_ref, growth_ref, damping_ref, cosine_ref, start_ref, high_ref, low_ref
+):
     shape = start_ref.shape
+    cosine = jnp.broadcast_to(cosine_ref[...], shape)
+    slots = shape[0]
+    wide = block_rows // 2 * slots
 
     def advance(index, carry):
         before, current, log_scale = carry
         scale = jnp.exp(log_scale)
         growth = growth_ref[index]
         damping = damping_ref[index]
+        rows = []
         for offset in range(block_rows):
-            row = current * scale
-            high = row.astype(jnp.bfloat16)
-            low = (row - high.astype(jnp.float32)).astype(jnp.bfloat16)
-            place = index * (block_rows // 2) + offset // 2
-            high_ref[offset % 2, place] = high
-            low_ref[offset % 2, place] = low
+            rows.append(current * scale)
             advanced = growth[:, offset : offset + 1] * (
                 cosine * current - damping[:, offset : offset + 1] * before
             )
             before, current = current, advanced
+            if offset % 4 == 3:
+                for parity in range(2):
+                    pair = jnp.concatenate([rows[offset - 3 + parity], rows[offset - 1 + parity]])
+                    high, low = split_high_low(pair)
+                    first = pl.multiple_of(index * wide + offset // 4 * 2 * slots, 2 * slots)
+                    high_ref[parity, 0, pl.ds(first, 2 * slots)] = high
+                    low_ref[parity, 0, pl.ds(first, 2 * slots)] = low
         biggest = jnp.maximum(jnp.abs(before), jnp.abs(current))
         return before / biggest, current / biggest, log_scale + jnp.log(biggest)
 
     lax.fori_loop(
         0,
-        growth_ref.shape[0],
+        blocks_ref[pl.program_id(0)] * (order_tile // block_rows),
         advance,
         (jnp.zeros(shape, jnp.float32), jnp.ones(shape, jnp.float32), start_ref[...]),
     )
 
 
-def legendre_table(growth, damping, cosine, start_log):
+def legendre_table(blocks_used, growth, damping, cosine, start_log):
     blocks, slots, _ = growth.shape
     lats = cosine.shape[1]
-    half = blocks * block_rows // 2
-    out = jax.ShapeDtypeStruct((2, half, slots, lats), jnp.bfloat16)
-    coef_spec = pl.BlockSpec((blocks, slot_tile, block_rows), lambda i: (0, i, 0))
-    out_spec = pl.BlockSpec((2, half, slot_tile, lats), lambda i: (0, 0, i, 0))
-    size = 2 * half * slots * lats
+    rows = blocks * block_rows // 2 * slot_tile
+    tiles = slots // slot_tile
+    out = jax.ShapeDtypeStruct((2, tiles, rows, lats), jnp.bfloat16)
+    coef_spec = pl.BlockSpec((blocks, slot_tile, block_rows), lambda i, used: (0, i, 0))
+    out_spec = pl.BlockSpec((2, 1, rows, lats), lambda i, used: (0, i, 0, 0))
+    size = 2 * tiles * rows * lats
     return pl.pallas_call(
         table_kernel,
-        grid=(slots // slot_tile,),
-        in_specs=[
-            coef_spec,
-            coef_spec,
-            pl.BlockSpec((1, lats), lambda i: (0, 0)),
-            pl.BlockSpec((slot_tile, lats), lambda i: (i, 0)),
-        ],
-        out_specs=[out_spec, out_spec],
+        grid_spec=pltpu.PrefetchScalarGridSpec(
+            num_scalar_prefetch=1,
+            grid=(tiles,),
+            in_specs=[
+                coef_spec,
+                coef_spec,
+                pl.BlockSpec((1, lats), lambda i, used: (0, 0)),
+                pl.BlockSpec((slot_tile, lats), lambda i, used: (i, 0)),
+            ],
+            out_specs=[out_spec, out_spec],
+        ),
         out_shape=[out, out],
         cost_estimate=pl.CostEstimate(
             flops=10 * size, bytes_accessed=4 * size, transcendentals=size // 4
         ),
         name="legendre_table",
-    )(growth, damping, cosine, start_log)
+    )(blocks_used, growth, damping, cosine, start_log)
 
 
 def contract_kernel(
-    high_ref, low_ref, weight_high_ref, weight_low_ref, own_ref, limit_ref, out_ref, sums_ref
+    blocks_ref,
+    high_ref,
+    low_ref,
+    weight_high_ref,
+    weight_low_ref,
+    own_ref,
+    limit_ref,
+    out_ref,
+    sums_ref,
 ):
-    step = pl.program_id(0)
-    _, orders, slots, lats = high_ref.shape
+    tile = pl.program_id(0)
+    step = pl.program_id(1)
+    rows = high_ref.shape[2]
+    slots = own_ref.shape[0]
+    orders = rows // slots
     lane_tiles, _, lanes = sums_ref.shape
     levels, rows_own, order_total = out_ref.shape
-    own = own_ref[...] > 0.0
-    for parity in range(2):
-        high = high_ref[parity].reshape(orders * slots, lats)
-        low = low_ref[parity].reshape(orders * slots, lats)
-        full = (
-            product(high, weight_high_ref[parity])
-            + product(high, weight_low_ref[parity])
-            + product(low, weight_high_ref[parity])
-        )
-        picked = jnp.where(own[None], full.reshape(orders, slots, lane_tiles * lanes), 0.0)
-        summed = jnp.sum(picked, axis=1)
-        for tile in range(lane_tiles):
-            sums_ref[tile, pl.ds(step * 2 * orders + parity, orders, stride=2), :] = summed[
-                :, tile * lanes : (tile + 1) * lanes
-            ]
-
-    @pl.when(step == pl.num_programs(0) - 1)
+
+    @pl.when((tile == 0) & (step == 0))
     def _():
-        turned = jnp.concatenate([sums_ref[tile].T for tile in range(lane_tiles)], axis=0)
+        sums_ref[...] = jnp.zeros_like(sums_ref)
+
+    @pl.when(step < blocks_ref[tile])
+    def _():
+        own = own_ref[...] > 0.0
+        for parity in range(2):
+            full = (
+                product(high_ref[parity, 0], weight_high_ref[parity])
+                + product(high_ref[parity, 0], weight_low_ref[parity])
+                + product(low_ref[parity, 0], weight_high_ref[parity])
+            )
+            picked = jnp.where(own[None], full.reshape(orders, slots, lane_tiles * lanes), 0.0)
+            summed = jnp.sum(picked, axis=1)
+            for k in range(lane_tiles):
+                place = pl.ds(step * 2 * orders + parity, orders, stride=2)
+                sums_ref[k, place, :] += summed[:, k * lanes : (k + 1) * lanes]
+
+    @pl.when((tile == pl.num_programs(0) - 1) & (step == pl.num_programs(1) - 1))
+    def _():
+        turned = jnp.concatenate([sums_ref[k].T for k in range(lane_tiles)], axis=0)
         turned = turned[:, :order_total]
         order = lax.broadcasted_iota(jnp.int32, turned.shape, 1)
         turned = jnp.where(order < limit_ref[...], turned, 0.0)
@@ -272,33 +347,45 @@
             out_ref[level] = turned[level * rows_own : (level + 1) * rows_own]
 
 
-def contract_table(high, low, weight_high, weight_low, own, limit, levels, rows_own):
-    _, half, slots, lats = high.shape
+def contract_table(
+    blocks_used, high, low, weight_high, weight_low, own, limit, levels, rows_own
+):
+    _, tiles, rows, lats = high.shape
     columns = weight_high.shape[1]
-    tile = 20
-    table_spec = pl.BlockSpec((2, tile, slots, lats), lambda i: (0, i, 0, 0))
-    weight_spec = pl.BlockSpec((2, columns, lats), lambda i: (0, 0, 0))
+    block = order_tile // 2 * slot_tile
+    order_total = 2 * rows // slot_tile
+
+    def table_map(i, j, used):
+        return (0, i, jnp.maximum(jnp.minimum(j, used[i] - 1), 0), 0)
+
+    table_spec = pl.BlockSpec((2, 1, block, lats), table_map)
+    weight_spec = pl.BlockSpec((2, columns, lats), lambda i, j, used: (0, 0, 0))
     return pl.pallas_call(
         contract_kernel,
-        grid=(half // tile,),
-        in_specs=[
-            table_spec,
-            table_spec,
-            weight_spec,
-            weight_spec,
-            pl.BlockSpec((slots, columns), lambda i: (0, 0)),
-            pl.BlockSpec((columns, 1), lambda i: (0, 0)),
-        ],
-        out_specs=pl.BlockSpec((levels, rows_own, 2 * half), lambda i: (0, 0, 0)),
-        out_shape=jax.ShapeDtypeStruct((levels, rows_own, 2 * half), jnp.float32),
-        scratch_shapes=[pltpu.VMEM((columns // 128, round_up(2 * half, 128), 128), jnp.float32)],
+        grid_spec=pltpu.PrefetchScalarGridSpec(
+            num_scalar_prefetch=1,
+            grid=(tiles, rows // block),
+            in_specs=[
+                table_spec,
+                table_spec,
+                weight_spec,
+                weight_spec,
+                pl.BlockSpec((slot_tile, columns), lambda i, j, used: (i, 0)),
+                pl.BlockSpec((columns, 1), lambda i, j, used: (0, 0)),
+            ],
+            out_specs=pl.BlockSpec((levels, rows_own, order_total), lambda i, j, used: (0, 0, 0)),
+            scratch_shapes=[
+                pltpu.VMEM((columns // LANES, round_up(order_total, LANES), LANES), jnp.float32)
+            ],
+        ),
+        out_shape=jax.ShapeDtypeStruct((levels, rows_own, order_total), jnp.float32),
         cost_estimate=pl.CostEstimate(
-            flops=12 * half * slots * lats * columns,
-            bytes_accessed=8 * half * slots * lats,
+            flops=12 * tiles * rows * lats * columns,
+            bytes_accessed=8 * tiles * rows * lats,
             transcendentals=0,
         ),
         name="legendre_contract",
-    )(high, low, weight_high, weight_low, own, limit)
+    )(blocks_used, high, low, weight_high, weight_low, own, limit)
 
 
 def split_pair(values):
@@ -326,9 +413,18 @@
     half_lat = NLAT // 2
     lat_padded = round_up(half_lat, 128)
     slots_padded = round_up(slots_own, slot_tile)
-    padded_waves = jnp.pad(my_waves, (0, slots_padded - slots_own))
+    index = jnp.arange(slots_own, dtype=jnp.int32)
+    larger = (my_waves[None, :] > my_waves[:, None]) | (
+        (my_waves[None, :] == my_waves[:, None]) & (index[None, :] < index[:, None])
+    )
+    row_of_slot = jnp.sum(larger.astype(jnp.int32), axis=1) + (slots_padded - slots_own)
+    row_ids = jnp.arange(slots_padded, dtype=jnp.int32)
+    placed = row_of_slot[None, :] == row_ids[:, None]
+    padded_waves = M - jnp.sum(jnp.where(placed, M - my_waves[None, :], 0), axis=1)
+    longest = jnp.max((M - padded_waves).reshape(-1, slot_tile), axis=1)
+    blocks_used = jnp.maximum(-(-longest // order_tile), 0)
     table_high, table_low = legendre_table(
-        *legendre_setup(padded_waves, M, NLAT, half_lat, lat_padded)
+        blocks_used, *legendre_setup(padded_waves, M, NLAT, half_lat, lat_padded)
     )
 
     targets = lat_parts * groups
@@ -339,8 +435,8 @@
         ((0, 0), (0, rows_padded - rows_own)),
         constant_values=M,
     ).reshape(-1)
-    table = fourier_table(row_waves, NLON, jnp.arange(targets * rows_padded, dtype=jnp.int32) % 2)
-    table = table.reshape(-1, groups, NLON // groups).transpose(1, 0, 2)
+    turns = jnp.arange(targets * rows_padded, dtype=jnp.int32) % 2
+    table = fourier_table(row_waves, turns, groups, NLON // groups, NLON)
 
     advected = advect(tracer, wind_east, wind_north, first_row, NLAT)
     advected = lax.all_to_all(advected, GROUP, split_axis=0, concat_axis=0, tiled=True)
@@ -362,12 +458,11 @@
         ((0, 0), (0, columns - used), (0, lat_padded - half_lat)),
     )
     slot_of_column = jnp.arange(columns, dtype=jnp.int32) % rows_own // 2
-    own = (jnp.arange(slots_padded, dtype=jnp.int32)[:, None] == slot_of_column[None, :]).astype(
-        jnp.float32
-    )
-    limit = (M - my_waves)[slot_of_column][:, None]
+    column_of_row = slot_of_column[None, :, None] == index[None, None, :]
+    own = jnp.any(column_of_row & placed[:, None, :], axis=2).astype(jnp.float32)
+    limit = jnp.sum(jnp.where(column_of_row[0], M - my_waves[None, :], 0), axis=1)[:, None]
     result = contract_table(
-        table_high, table_low, *split_pair(folded), own, limit, levels, rows_own
+        blocks_used, table_high, table_low, *split_pair(folded), own, limit, levels, rows_own
     )
     result = lax.all_to_all(result, GROUP, split_axis=0, concat_axis=0, tiled=True)
     result = result.reshape(groups, own_levels, slots_own, 2, M).transpose(1, 0, 2, 3, 4)

time: 142 us -> 122 us (0.86)
  other arithmetic: 53.8 us -> 14 us
  waiting for transfers between devices: 0.02 us -> 11.6 us
  Pallas kernels: 47.8 us -> 55.3 us
    mul x3, other arithmetic: 30.2 us -> 2.46 us  [the longest x1 2.46 us: fourier_factors(): jnp.sin(base) * factor]
    gather x20 -> x0, other arithmetic: 16.5 us -> none  [shards(): limit = (M - my_waves)[slot_of_column][:, None]]
    all_to_all x1, waiting for transfers between devices: 0.01 us -> 11 us  [shards(): lax.all_to_all(advected, GROUP, split_axis=0, concat_axis=0, tiled=True)]
    pallas_call x2 -> x3, Pallas kernels: 35.7 us -> 42.9 us  [the longest x1 19.6 us: contract_table(): pl.pallas_call(contract_kernel, grid_spec=pltpu.PrefetchScalarGridSpec(nu...]
    sin x0 -> x1, other arithmetic: none -> 3.08 us  [fourier_factors(): jnp.sin(lane)]
  transfers between devices with their start and end apart: 6 -> 6, of which waited for: 0 -> 2; matrix products, arithmetic and copies ran while one was open for 41% -> 14% of each run, Pallas kernels for 13% -> 19%
where the time goes in v3:
time: 122 us; the launch traced here: 120 us
  Pallas kernels  55.3 us (45%)
  starting transfers between devices  15.7 us (13%)
  other arithmetic  14 us (11%)
  blocking collectives  11.8 us (10%)
  waiting for transfers between devices  11.6 us (10%)
  local copies, waits for them, and re-layouts  11.2 us (9%)
    pallas_call x1, Pallas kernels, contract_table(): pl.pallas_call(contract_kernel, grid_spec=pltpu.PrefetchScalarGridSpec(nu...  19.6 us
    pallas_call x1, Pallas kernels, legendre_table(): pl.pallas_call(table_kernel, grid_spec=pltpu.PrefetchScalarGridSpec(num_s...  15 us
    all_to_all x1, blocking collectives, shards(): lax.all_to_all(result, GROUP, split_axis=0, concat_axis=0, tiled=True)  11.8 us
    all_to_all x1, waiting for transfers between devices, shards(): lax.all_to_all(advected, GROUP, split_axis=0, concat_axis=0, tiled=True)  11 us
    pallas_call x1, Pallas kernels, fourier_table(): pl.pallas_call(wave_table_kernel, grid=(rows // tall,), in_specs=[pl.Bloc...  8.36 us
    pallas_call x1, Pallas kernels, fourier_transform(): pl.pallas_call(lambda *refs: fourier_kernel(rows_own, *refs), grid=(chunk...  7.75 us
    ppermute x2, starting transfers between devices, edges(): high = lax.ppermute(lax.slice_in_dim(block, 0, 1, axis=dim), axis, backward)  6.86 us
    all_to_all x1, starting transfers between devices, shards(): lax.all_to_all(fourier, ('lat',) + GROUP, split_axis=0, concat_axis=0, ti...  5.2 us
  transfers between devices with their start and end apart: 6, of which 2 were waited for; matrix products, arithmetic and copies ran while one was open for 14% of the time, Pallas kernels for 19%

profile of v3, /device:TPU:0, one launch (start us, length us, event | category | flops | bytes accessed | tf_op | source)
XLA Modules:
  0.0 119.9 jit_solution(1690982869077750300)
XLA Ops:
  0.0 0.8 fusion.31
  0.8 5.1 %collective-permute-start.3 = (bf16[4,1,400]{2,1,0:T(2,128)(2,1)S(1)}, bf16[4,1,400]{2,1,0:T(2,128)(2,1)S(1)}, u32[]{:S(2)}, u32[]{:S(2)}) collective-permute-start(bf16[4,1,400]{2,1,0:T(2,128)(2,1)S(1)} %get-tuple-element.19), channel_id=1, source_target_pairs={{4,0},{8,4},{12,8},{0,12},{5,1},{9,5},{13,9},{1,13},{6,2},{10,6},{... | collective-permute-start | bytes 9608 | tf_op jit(solution)/shard_map/ppermute | solution.py:32
  5.9 0.0 collective-permute-start.2
  5.9 1.2 fusion.32
  7.1 0.1 collective-permute-start
  7.2 1.7 %collective-permute-start.1 = (bf16[4,200,1]{2,1,0:T(8,128)(2,1)S(1)}, bf16[4,200,1]{2,1,0:T(8,128)(2,1)S(1)}, u32[]{:S(2)}, u32[]{:S(2)}) collective-permute-start(bf16[4,200,1]{2,1,0:T(8,128)(2,1)S(1)} %get-tuple-element.21), channel_id=1, source_target_pairs={{1,0},{2,1},{3,2},{0,3},{5,4},{6,5},{7,6},{4,7},{9,8},{10,9},{11,1... | collective-permute-start | bytes 4808 | tf_op jit(solution)/shard_map/ppermute | solution.py:32
  8.9 0.8 reshape_reshape.3
  9.7 0.1 copy.25
  9.8 0.1 copy.34
  9.9 0.1 mul.234
  10.0 0.1 broadcast_add_fusion
  10.1 0.1 add.214
  10.2 3.1 %fusion.8 = (f32[896,128]{1,0:T(8,128)}, f32[896,128]{1,0:T(8,128)}) fusion(s32[896]{0:T(1024)S(1)} %mul.234), kind=kLoop, calls=%fused_computation.20 | loop fusion | flops 1032192 | bytes 921088 | tf_op jit(solution)/shard_map/sin | solution.py:44
  13.2 0.1 fusion.20
  13.4 0.2 copy.27
  13.6 2.5 %sine_multiply_fusion = (f32[896,16]{1,0:T(8,128)}, f32[896,16]{1,0:T(8,128)}) fusion(f32[896,16]{1,0:T(8,128)S(1)} %copy.27), kind=kLoop, calls=%fused_computation.22 | loop fusion | flops 43008 | bytes 172032 | tf_op jit(solution)/shard_map/mul | solution.py:44
  16.0 0.8 broadcast_subtract_fusion
  16.8 0.2 convert_reduce_fusion
  17.0 0.1 select_reduce_fusion.2
  17.1 0.0 collective-permute-done.3
  17.2 0.6 convert_multiply_fusion.below_ref
  17.8 0.0 collective-permute-done.2
  17.8 0.6 convert_multiply_fusion.1.above_ref
  18.4 0.0 collective-permute-done.west_ref
  18.4 0.0 copy-start.1
  18.4 0.0 collective-permute-done.1.east_ref
  18.4 0.7 copy-done.1
  19.0 0.0 copy-start.2
  19.0 0.7 copy-done.2
  19.7 4.6 %advect.1 = f32[4,200,400]{2,1,0:T(8,128)} custom-call(bf16[4,200,400]{2,1,0:T(8,128)(2,1)} %tracer_ref.1, bf16[4,200,400]{2,1,0:T(8,128)(2,1)} %east_wind_ref.1, bf16[4,200,400]{2,1,0:T(8,128)(2,1)} %north_wind_ref.1, bf16[4,200,1]{2,1,0:T(8,128)(2,1)} %copy-done.1, bf16[4,200,1]{2,1,0:T(8,128)(2,1)} %copy-done.2, ...), custom_call_target="tpu_custom_call" | custom-call | flops 3200000 | bytes 3200000 | tf_op jit(solution)/shard_map/advect/pallas_call | solution.py:119
  24.3 3.6 %all-to-all-start = ((f32[4,200,400]{2,1,0:T(8,128)}), f32[4,200,400]{2,1,0:T(8,128)S(1)}, u32[]{:S(2)}, u32[]{:S(2)}) async-start(f32[4,200,400]{2,1,0:T(8,128)} %advect.1), calls=%async_computation | async-start | bytes 3276800 | tf_op jit(solution)/shard_map/all_to_all | solution.py:442
  27.9 1.0 broadcast_in_dim_reshape.3.refs_3_
  28.9 0.1 copy.31
  29.0 8.4 %fourier_table.1 = (bf16[4,896,512]{2,1,0:T(8,128)(2,1)}, bf16[4,896,512]{2,1,0:T(8,128)(2,1)}) custom-call(f32[896,16]{1,0:T(8,128)} %get-tuple-element.24.base_cos_ref, f32[896,16]{1,0:T(8,128)} %get-tuple-element.23.base_sin_ref, f32[896,128]{1,0:T(8,128)} %get-tuple-element.28.lane_cos_ref, f32[896,128]{1,0:T(8,128)} %get-tuple-element.27.lane_sin_ref), custom_call_target="tpu_custom_call" | custom-call | flops 14680064 | bytes 7340032 | tf_op jit(solution)/shard_map/fourier_table/pallas_call | solution.py:75
  37.4 0.1 select_reduce_fusion.1
  37.5 0.2 and_reduce_fusion
  37.7 11.0 %all-to-all-done = f32[4,200,400]{2,1,0:T(8,128)S(1)} async-done(((f32[4,200,400]{2,1,0:T(8,128)}), f32[4,200,400]{2,1,0:T(8,128)S(1)}, u32[]{:S(2)}, u32[]{:S(2)}) %all-to-all-start) | async-done | bytes 1280032 | tf_op jit(solution)/shard_map/all_to_all | solution.py:442
  48.6 0.0 copy-start
  48.6 1.3 %copy-done = f32[4,200,400]{2,1,0:T(8,128)} copy-done((f32[4,200,400]{2,1,0:T(8,128)}, f32[4,200,400]{2,1,0:T(8,128)S(1)}, u32[]{:S(2)}) %copy-start) | copy-done | bytes 1280024
  49.9 7.8 %fourier_transform.1 = f32[16,50,200]{2,1,0:T(8,128)} custom-call(bf16[4,896,512]{2,1,0:T(8,128)(2,1)} %get-tuple-element.11.refs_0_, bf16[4,896,512]{2,1,0:T(8,128)(2,1)} %get-tuple-element.12.refs_1_, f32[4,1,200,400]{3,2,1,0:T(8,128)} %bitcast.11, s32[896,1]{1,0:T(8,128)} %broadcast_in_dim_reshape.3.refs_3_, s32[1,200]{1,0:T(1,128)} %bitcast.15), custom_call_target="tpu_custom_call" | custom-call | flops 1720320000 | bytes 5734400 | tf_op jit(solution)/shard_map/fourier_transform/pallas_call | solution.py:185
  57.7 5.2 %all-to-all-start.1 = ((f32[16,50,200]{2,1,0:T(8,128)}), f32[16,50,200]{2,1,0:T(8,128)S(1)}, u32[]{:S(2)}, u32[]{:S(2)}) async-start(f32[16,50,200]{2,1,0:T(8,128)} %fourier_transform.1), calls=%async_computation.1 | async-start | bytes 1835008 | tf_op jit(solution)/shard_map/all_to_all | solution.py:445
  62.9 0.7 multiply_cosine_fusion.cosine_ref
  63.5 0.1 reshape.219
  63.6 0.8 copy.32.limit_ref
  64.4 0.6 convert_element_type.71.own_ref
  65.1 0.1 reduce_max.9
  65.2 0.2 select_reduce_fusion
  65.4 0.6 negate_maximum_fusion.blocks_ref
  65.9 0.7 multiply_add_fusion.start_ref
  66.6 1.4 %fusion.13 = (f32[25,32,16]{2,1,0:T(8,128)}, f32[25,32,16]{2,1,0:T(8,128)}) fusion(f32[32]{0:T(128)S(1)} %minimum_convert_fusion, f32[32]{0:T(128)S(1)} %fusion.30, f32[25,16]{1,0:T(8,128)S(1)} %add_add_fusion.1), kind=kLoop, calls=%fused_computation.27 | loop fusion | flops 192000 | bytes 104256 | tf_op jit(solution)/shard_map/sqrt | solution.py:224
  68.0 15.0 %legendre_table.1 = (bf16[2,4,1600,512]{3,2,1,0:T(8,128)(2,1)}, bf16[2,4,1600,512]{3,2,1,0:T(8,128)(2,1)}) custom-call(s32[4]{0:T(128)} %negate_maximum_fusion.blocks_ref, f32[25,32,16]{2,1,0:T(8,128)} %get-tuple-element.26.growth_ref, f32[25,32,16]{2,1,0:T(8,128)} %get-tuple-element.25.damping_ref, f32[1,512]{1,0:T(1,128)} %multiply_cosine_fusion.cosine_ref, ...), custom_call_target="tpu_custom_call" | custom-call | flops 65536000 | bytes 26214400 | tf_op jit(solution)/shard_map/legendre_table/pallas_call | solution.py:281
  83.0 0.6 all-to-all-done.1
  83.7 0.1 reshape.222
  83.8 0.3 copy.30
  84.1 0.5 reshape.223
  84.6 0.1 broadcast_multiply_fusion
  84.6 0.2 slice.25
  84.8 1.3 %reverse = f32[200,512]{1,0:T(8,128)S(1)} reverse(f32[200,512]{1,0:T(8,128)S(1)} %bitcast.13), dimensions={1} | reverse | bytes 819200
  86.1 0.2 add_bitcast_fusion
  86.3 1.1 fusion
  87.4 19.6 %legendre_contract.1 = f32[4,50,400]{2,1,0:T(8,128)} custom-call(s32[4]{0:T(128)} %negate_maximum_fusion.blocks_ref, bf16[2,4,1600,512]{3,2,1,0:T(8,128)(2,1)} %get-tuple-element.9.high_ref, bf16[2,4,1600,512]{3,2,1,0:T(8,128)(2,1)} %get-tuple-element.10.low_ref, bf16[2,256,512]{2,1,0:T(8,128)(2,1)} %get-tuple-element.18.weight_high_ref, ...), custom_call_target="tpu_custom_call" | custom-call | flops 10066329600 | bytes 26214400 | tf_op jit(solution)/shard_map/legendre_contract/pallas_call | solution.py:363
  107.0 11.8 %all_to_all.15 = f32[4,50,400]{2,1,0:T(8,128)S(1)} all-to-all(f32[4,50,400]{2,1,0:T(8,128)} %legendre_contract.1), channel_id=1, replica_groups=mesh['member'=2,'lat'=4,'lev'=2,'fld'=2] {'lev','fld'}, dimensions={0} | all-to-all | bytes 640000 | tf_op jit(solution)/shard_map/all_to_all | solution.py:467
  118.9 1.0 reshape_transpose_reshape.3
  (17 shorter events, 0.3 us)
Async XLA Ops:
  0.8 16.4 %collective-permute-start.3 = (bf16[4,1,400]{2,1,0:T(2,128)(2,1)S(1)}, bf16[4,1,400]{2,1,0:T(2,128)(2,1)S(1)}, u32[]{:S(2)}, u32[]{:S(2)}) collective-permute-start(bf16[4,1,400]{2,1,0:T(2,128)(2,1)S(1)} %get-tuple-element.19), channel_id=1, source_target_pairs={{4,0},{8,4},{12,8},{0,12},{5,1},{9,5},{13,9},{1,13},{6,2},{10,6},{... | collective-permute-start | bytes 9608 | tf_op jit(solution)/shard_map/ppermute | solution.py:32
  5.9 11.8 %collective-permute-start.2 = (bf16[4,1,400]{2,1,0:T(2,128)(2,1)S(1)}, bf16[4,1,400]{2,1,0:T(2,128)(2,1)S(1)}, u32[]{:S(2)}, u32[]{:S(2)}) collective-permute-start(bf16[4,1,400]{2,1,0:T(2,128)(2,1)S(1)} %get-tuple-element.20), channel_id=1, source_target_pairs={{0,4},{4,8},{8,12},{12,0},{1,5},{5,9},{9,13},{13,1},{2,6},{6,10},{... | collective-permute-start | bytes 9608 | tf_op jit(solution)/shard_map/ppermute | solution.py:29
  7.1 11.3 %collective-permute-start = (bf16[4,200,1]{2,1,0:T(8,128)(2,1)S(1)}, bf16[4,200,1]{2,1,0:T(8,128)(2,1)S(1)}, u32[]{:S(2)}, u32[]{:S(2)}) collective-permute-start(bf16[4,200,1]{2,1,0:T(8,128)(2,1)S(1)} %get-tuple-element.22), channel_id=1, source_target_pairs={{0,1},{1,2},{2,3},{3,0},{4,5},{5,6},{6,7},{7,4},{8,9},{9,10},{10,1... | collective-permute-start | bytes 4808 | tf_op jit(solution)/shard_map/ppermute | solution.py:29
  7.2 11.2 %collective-permute-start.1 = (bf16[4,200,1]{2,1,0:T(8,128)(2,1)S(1)}, bf16[4,200,1]{2,1,0:T(8,128)(2,1)S(1)}, u32[]{:S(2)}, u32[]{:S(2)}) collective-permute-start(bf16[4,200,1]{2,1,0:T(8,128)(2,1)S(1)} %get-tuple-element.21), channel_id=1, source_target_pairs={{1,0},{2,1},{3,2},{0,3},{5,4},{6,5},{7,6},{4,7},{9,8},{10,9},{11,1... | collective-permute-start | bytes 4808 | tf_op jit(solution)/shard_map/ppermute | solution.py:32
  18.4 0.7 copy-start.1
  19.0 0.7 copy-start.2
  24.3 24.3 %all-to-all-start = ((f32[4,200,400]{2,1,0:T(8,128)}), f32[4,200,400]{2,1,0:T(8,128)S(1)}, u32[]{:S(2)}, u32[]{:S(2)}) async-start(f32[4,200,400]{2,1,0:T(8,128)} %advect.1), calls=%async_computation | async-start | bytes 3276800 | tf_op jit(solution)/shard_map/all_to_all | solution.py:442
  48.6 1.3 %copy-start = (f32[4,200,400]{2,1,0:T(8,128)}, f32[4,200,400]{2,1,0:T(8,128)S(1)}, u32[]{:S(2)}) copy-start(f32[4,200,400]{2,1,0:T(8,128)S(1)} %all-to-all-done) | copy-start | bytes 3840004
  57.7 26.0 %all-to-all-start.1 = ((f32[16,50,200]{2,1,0:T(8,128)}), f32[16,50,200]{2,1,0:T(8,128)S(1)}, u32[]{:S(2)}, u32[]{:S(2)}) async-start(f32[16,50,200]{2,1,0:T(8,128)} %fourier_transform.1), calls=%async_computation.1 | async-start | bytes 1835008 | tf_op jit(solution)/shard_map/all_to_all | solution.py:445

commit v4 on v3

--- a/solution.py
+++ b/solution.py
@@ -135,27 +135,32 @@
     return high, (values - high.astype(jnp.float32)).astype(jnp.bfloat16)
 
 
-def product(left, right):
-    return lax.dot_general(
-        left, right, (((1,), (1,)), ((), ())), preferred_element_type=jnp.float32
-    )
+def three_passes(high, low):
+    return jnp.concatenate([high, high, low], axis=1)
+
+
+def turned_passes(values):
+    high, low = split_high_low(values.T)
+    return jnp.concatenate([high, low, high], axis=0)
 
 
 def fourier_kernel(
-    rows_own, table_high_ref, table_low_ref, field_ref, wave_ref, keep_ref, out_ref, total_ref
+    rows_own, table_high_ref, table_low_ref, field_ref, wave_ref, keep_ref, out_ref, total_ref, pad_ref
 ):
     step = pl.program_id(0)
     _, levels, lat_rows, lons = field_ref.shape
     targets = out_ref.shape[0]
     rows_padded = table_high_ref.shape[1] // targets
-    table_high = table_high_ref[0][:, :lons]
-    table_low = table_low_ref[0][:, :lons]
+    table = three_passes(table_high_ref[0], table_low_ref[0])
+
+    @pl.when(step == 0)
+    def _():
+        pad_ref[...] = jnp.zeros_like(pad_ref)
+
     for level in range(levels):
-        field_high, field_low = split_high_low(field_ref[0, level])
-        term = (
-            product(table_high, field_high)
-            + product(table_high, field_low)
-            + product(table_low, field_high)
+        pad_ref[:lat_rows, :lons] = field_ref[0, level]
+        term = jnp.dot(
+            table, turned_passes(pad_ref[...]), preferred_element_type=jnp.float32
         )
 
         @pl.when(step == 0)
@@ -170,7 +175,7 @@
     def _():
         kept = wave_ref[...] < keep_ref[...]
         for level in range(levels):
-            masked = jnp.where(kept, total_ref[level], 0.0)
+            masked = jnp.where(kept, total_ref[level][:, :lat_rows], 0.0)
             for target in range(targets):
                 first = target * rows_padded
                 out_ref[target, level * rows_own : (level + 1) * rows_own] = masked[
@@ -194,7 +199,10 @@
         ],
         out_specs=pl.BlockSpec((targets, levels * rows_own, lat_rows), lambda i: (0, 0, 0)),
         out_shape=jax.ShapeDtypeStruct((targets, levels * rows_own, lat_rows), jnp.float32),
-        scratch_shapes=[pltpu.VMEM((levels, rows, lat_rows), jnp.float32)],
+        scratch_shapes=[
+            pltpu.VMEM((levels, rows, round_up(lat_rows, LANES)), jnp.float32),
+            pltpu.VMEM((round_up(lat_rows, LANES), table[0].shape[2]), jnp.float32),
+        ],
         cost_estimate=pl.CostEstimate(
             flops=6 * rows * chunks * levels * lat_rows * lons,
             bytes_accessed=4 * rows * chunks * lons,
@@ -303,43 +311,50 @@
     blocks_ref,
     high_ref,
     low_ref,
-    weight_high_ref,
-    weight_low_ref,
+    folded_ref,
     own_ref,
     limit_ref,
     out_ref,
+    weight_ref,
     sums_ref,
+    mixed_ref,
 ):
     tile = pl.program_id(0)
     step = pl.program_id(1)
     rows = high_ref.shape[2]
     slots = own_ref.shape[0]
     orders = rows // slots
-    lane_tiles, _, lanes = sums_ref.shape
+    _, lane_tiles, half, lanes = sums_ref.shape
     levels, rows_own, order_total = out_ref.shape
 
     @pl.when((tile == 0) & (step == 0))
     def _():
         sums_ref[...] = jnp.zeros_like(sums_ref)
+        mixed_ref[...] = jnp.zeros_like(mixed_ref)
+        for parity in range(2):
+            weight_ref[parity] = turned_passes(folded_ref[parity])
 
     @pl.when(step < blocks_ref[tile])
     def _():
         own = own_ref[...] > 0.0
         for parity in range(2):
-            full = (
-                product(high_ref[parity, 0], weight_high_ref[parity])
-                + product(high_ref[parity, 0], weight_low_ref[parity])
-                + product(low_ref[parity, 0], weight_high_ref[parity])
+            full = jnp.dot(
+                three_passes(high_ref[parity, 0], low_ref[parity, 0]),
+                weight_ref[parity],
+                preferred_element_type=jnp.float32,
             )
             picked = jnp.where(own[None], full.reshape(orders, slots, lane_tiles * lanes), 0.0)
             summed = jnp.sum(picked, axis=1)
             for k in range(lane_tiles):
-                place = pl.ds(step * 2 * orders + parity, orders, stride=2)
-                sums_ref[k, place, :] += summed[:, k * lanes : (k + 1) * lanes]
+                place = pl.ds(pl.multiple_of(step * orders, 8), orders)
+                sums_ref[parity, k, place, :] += summed[:, k * lanes : (k + 1) * lanes]
 
     @pl.when((tile == pl.num_programs(0) - 1) & (step == pl.num_programs(1) - 1))
     def _():
-        turned = jnp.concatenate([sums_ref[k].T for k in range(lane_tiles)], axis=0)
+        for parity in range(2):
+            for k in range(lane_tiles):
+                mixed_ref[k, pl.ds(parity, half, stride=2), :] = sums_ref[parity, k]
+        turned = jnp.concatenate([mixed_ref[k].T for k in range(lane_tiles)], axis=0)
         turned = turned[:, :order_total]
         order = lax.broadcasted_iota(jnp.int32, turned.shape, 1)
         turned = jnp.where(order < limit_ref[...], turned, 0.0)
@@ -348,10 +363,10 @@
 
 
 def contract_table(
-    blocks_used, high, low, weight_high, weight_low, own, limit, levels, rows_own
+    blocks_used, high, low, folded, own, limit, levels, rows_own
 ):
     _, tiles, rows, lats = high.shape
-    columns = weight_high.shape[1]
+    columns = folded.shape[1]
     block = order_tile // 2 * slot_tile
     order_total = 2 * rows // slot_tile
 
@@ -369,13 +384,14 @@
                 table_spec,
                 table_spec,
                 weight_spec,
-                weight_spec,
                 pl.BlockSpec((slot_tile, columns), lambda i, j, used: (i, 0)),
                 pl.BlockSpec((columns, 1), lambda i, j, used: (0, 0)),
             ],
             out_specs=pl.BlockSpec((levels, rows_own, order_total), lambda i, j, used: (0, 0, 0)),
             scratch_shapes=[
-                pltpu.VMEM((columns // LANES, round_up(order_total, LANES), LANES), jnp.float32)
+                pltpu.VMEM((2, 3 * lats, columns), jnp.bfloat16),
+                pltpu.VMEM((2, columns // LANES, order_total // 2, LANES), jnp.float32),
+                pltpu.VMEM((columns // LANES, round_up(order_total, LANES), LANES), jnp.float32),
             ],
         ),
         out_shape=jax.ShapeDtypeStruct((levels, rows_own, order_total), jnp.float32),
@@ -385,12 +401,7 @@
             transcendentals=0,
         ),
         name="legendre_contract",
-    )(blocks_used, high, low, weight_high, weight_low, own, limit)
-
-
-def split_pair(values):
-    high = lax.reduce_precision(values, 8, 7)
-    return high.astype(jnp.bfloat16), (values - high).astype(jnp.bfloat16)
+    )(blocks_used, high, low, folded, own, limit)
 
 
 def shards(tracer, wind_east, wind_north, keep_m, slot_wave):
@@ -462,7 +473,7 @@
     own = jnp.any(column_of_row & placed[:, None, :], axis=2).astype(jnp.float32)
     limit = jnp.sum(jnp.where(column_of_row[0], M - my_waves[None, :], 0), axis=1)[:, None]
     result = contract_table(
-        blocks_used, table_high, table_low, *split_pair(folded), own, limit, levels, rows_own
+        blocks_used, table_high, table_low, folded, own, limit, levels, rows_own
     )
     result = lax.all_to_all(result, GROUP, split_axis=0, concat_axis=0, tiled=True)
     result = result.reshape(groups, own_levels, slots_own, 2, M).transpose(1, 0, 2, 3, 4)

time: 122 us -> 123 us (level)
  no operation moved by 1% of the time
where the time goes in v4:
time: 123 us; the launch traced here: 122 us
  Pallas kernels  56.1 us (46%)
  starting transfers between devices  15.7 us (13%)
  other arithmetic  14 us (11%)
  blocking collectives  12.9 us (10%)
  waiting for transfers between devices  11.7 us (10%)
  local copies, waits for them, and re-layouts  11.2 us (9%)
    pallas_call x1, Pallas kernels, contract_table(): pl.pallas_call(contract_kernel, grid_spec=pltpu.PrefetchScalarGridSpec(nu...  19.7 us
    pallas_call x1, Pallas kernels, legendre_table(): pl.pallas_call(table_kernel, grid_spec=pltpu.PrefetchScalarGridSpec(num_s...  15 us
    all_to_all x1, blocking collectives, shards(): lax.all_to_all(result, GROUP, split_axis=0, concat_axis=0, tiled=True)  12.9 us
    all_to_all x1, waiting for transfers between devices, shards(): lax.all_to_all(advected, GROUP, split_axis=0, concat_axis=0, tiled=True)  11 us
    pallas_call x1, Pallas kernels, fourier_transform(): pl.pallas_call(lambda *refs: fourier_kernel(rows_own, *refs), grid=(chunk...  8.47 us
    pallas_call x1, Pallas kernels, fourier_table(): pl.pallas_call(wave_table_kernel, grid=(rows // tall,), in_specs=[pl.Bloc...  8.36 us
    ppermute x2, starting transfers between devices, edges(): high = lax.ppermute(lax.slice_in_dim(block, 0, 1, axis=dim), axis, backward)  6.86 us
    all_to_all x1, starting transfers between devices, shards(): lax.all_to_all(fourier, ('lat',) + GROUP, split_axis=0, concat_axis=0, ti...  5.2 us
  transfers between devices with their start and end apart: 6, of which 2 were waited for; matrix products, arithmetic and copies ran while one was open for 14% of the time, Pallas kernels for 19%

profile of v4, /device:TPU:0, one launch (start us, length us, event | category | flops | bytes accessed | tf_op | source)
XLA Modules:
  0.0 121.7 jit_solution(14902849719166816539)
XLA Ops:
  0.0 0.8 fusion.30
  0.8 5.1 %collective-permute-start.3 = (bf16[4,1,400]{2,1,0:T(2,128)(2,1)S(1)}, bf16[4,1,400]{2,1,0:T(2,128)(2,1)S(1)}, u32[]{:S(2)}, u32[]{:S(2)}) collective-permute-start(bf16[4,1,400]{2,1,0:T(2,128)(2,1)S(1)} %get-tuple-element.17), channel_id=1, source_target_pairs={{4,0},{8,4},{12,8},{0,12},{5,1},{9,5},{13,9},{1,13},{6,2},{10,6},{... | collective-permute-start | bytes 9608 | tf_op jit(solution)/shard_map/ppermute | solution.py:32
  5.9 0.0 collective-permute-start.2
  5.9 1.2 fusion.31
  7.1 0.1 collective-permute-start
  7.2 1.7 %collective-permute-start.1 = (bf16[4,200,1]{2,1,0:T(8,128)(2,1)S(1)}, bf16[4,200,1]{2,1,0:T(8,128)(2,1)S(1)}, u32[]{:S(2)}, u32[]{:S(2)}) collective-permute-start(bf16[4,200,1]{2,1,0:T(8,128)(2,1)S(1)} %get-tuple-element.19), channel_id=1, source_target_pairs={{1,0},{2,1},{3,2},{0,3},{5,4},{6,5},{7,6},{4,7},{9,8},{10,9},{11,1... | collective-permute-start | bytes 4808 | tf_op jit(solution)/shard_map/ppermute | solution.py:32
  8.9 0.8 reshape_reshape.3
  9.7 0.1 copy.25
  9.8 0.1 copy.34
  9.9 0.1 mul.234
  10.0 0.1 broadcast_add_fusion
  10.1 0.1 add.214
  10.2 3.1 %fusion.7 = (f32[896,128]{1,0:T(8,128)}, f32[896,128]{1,0:T(8,128)}) fusion(s32[896]{0:T(1024)S(1)} %mul.234), kind=kLoop, calls=%fused_computation.17 | loop fusion | flops 1032192 | bytes 921088 | tf_op jit(solution)/shard_map/sin | solution.py:44
  13.2 0.1 fusion.19
  13.3 0.2 copy.27
  13.5 2.5 %sine_multiply_fusion = (f32[896,16]{1,0:T(8,128)}, f32[896,16]{1,0:T(8,128)}) fusion(f32[896,16]{1,0:T(8,128)S(1)} %copy.27), kind=kLoop, calls=%fused_computation.19 | loop fusion | flops 43008 | bytes 172032 | tf_op jit(solution)/shard_map/mul | solution.py:44
  16.0 0.8 broadcast_subtract_fusion
  16.8 0.2 convert_reduce_fusion
  17.0 0.1 select_reduce_fusion.2
  17.1 0.0 collective-permute-done.3
  17.2 0.6 convert_multiply_fusion.below_ref
  17.8 0.0 collective-permute-done.2
  17.8 0.6 convert_multiply_fusion.1.above_ref
  18.4 0.0 collective-permute-done.west_ref
  18.4 0.0 copy-start.1
  18.4 0.0 collective-permute-done.1.east_ref
  18.4 0.7 copy-done.1
  19.1 0.0 copy-start.2
  19.1 0.7 copy-done.2
  19.7 4.6 %advect.1 = f32[4,200,400]{2,1,0:T(8,128)} custom-call(bf16[4,200,400]{2,1,0:T(8,128)(2,1)} %tracer_ref.1, bf16[4,200,400]{2,1,0:T(8,128)(2,1)} %east_wind_ref.1, bf16[4,200,400]{2,1,0:T(8,128)(2,1)} %north_wind_ref.1, bf16[4,200,1]{2,1,0:T(8,128)(2,1)} %copy-done.1, bf16[4,200,1]{2,1,0:T(8,128)(2,1)} %copy-done.2, ...), custom_call_target="tpu_custom_call" | custom-call | flops 3200000 | bytes 3200000 | tf_op jit(solution)/shard_map/advect/pallas_call | solution.py:119
  24.3 3.6 %all-to-all-start = ((f32[4,200,400]{2,1,0:T(8,128)}), f32[4,200,400]{2,1,0:T(8,128)S(1)}, u32[]{:S(2)}, u32[]{:S(2)}) async-start(f32[4,200,400]{2,1,0:T(8,128)} %advect.1), calls=%async_computation | async-start | bytes 3276800 | tf_op jit(solution)/shard_map/all_to_all | solution.py:453
  27.9 1.0 broadcast_in_dim_reshape.3.refs_3_
  28.9 0.1 copy.31
  29.0 8.4 %fourier_table.1 = (bf16[4,896,512]{2,1,0:T(8,128)(2,1)}, bf16[4,896,512]{2,1,0:T(8,128)(2,1)}) custom-call(f32[896,16]{1,0:T(8,128)} %get-tuple-element.22.base_cos_ref, f32[896,16]{1,0:T(8,128)} %get-tuple-element.21.base_sin_ref, f32[896,128]{1,0:T(8,128)} %get-tuple-element.26.lane_cos_ref, f32[896,128]{1,0:T(8,128)} %get-tuple-element.25.lane_sin_ref), custom_call_target="tpu_custom_call" | custom-call | flops 14680064 | bytes 7340032 | tf_op jit(solution)/shard_map/fourier_table/pallas_call | solution.py:75
  37.3 0.1 select_reduce_fusion.1
  37.4 0.2 and_reduce_fusion
  37.6 11.0 %all-to-all-done = f32[4,200,400]{2,1,0:T(8,128)S(1)} async-done(((f32[4,200,400]{2,1,0:T(8,128)}), f32[4,200,400]{2,1,0:T(8,128)S(1)}, u32[]{:S(2)}, u32[]{:S(2)}) %all-to-all-start) | async-done | bytes 1280032 | tf_op jit(solution)/shard_map/all_to_all | solution.py:453
  48.6 0.0 copy-start
  48.6 1.3 %copy-done = f32[4,200,400]{2,1,0:T(8,128)} copy-done((f32[4,200,400]{2,1,0:T(8,128)}, f32[4,200,400]{2,1,0:T(8,128)S(1)}, u32[]{:S(2)}) %copy-start) | copy-done | bytes 1280024
  49.9 8.5 %fourier_transform.1 = f32[16,50,200]{2,1,0:T(8,128)} custom-call(bf16[4,896,512]{2,1,0:T(8,128)(2,1)} %get-tuple-element.11.refs_0_, bf16[4,896,512]{2,1,0:T(8,128)(2,1)} %get-tuple-element.12.refs_1_, f32[4,1,200,400]{3,2,1,0:T(8,128)} %bitcast.11, s32[896,1]{1,0:T(8,128)} %broadcast_in_dim_reshape.3.refs_3_, s32[1,200]{1,0:T(1,128)} %bitcast.15), custom_call_target="tpu_custom_call" | custom-call | flops 1720320000 | bytes 5734400 | tf_op jit(solution)/shard_map/fourier_transform/pallas_call | solution.py:190
  58.3 5.2 %all-to-all-start.1 = ((f32[16,50,200]{2,1,0:T(8,128)}), f32[16,50,200]{2,1,0:T(8,128)S(1)}, u32[]{:S(2)}, u32[]{:S(2)}) async-start(f32[16,50,200]{2,1,0:T(8,128)} %fourier_transform.1), calls=%async_computation.1 | async-start | bytes 1835008 | tf_op jit(solution)/shard_map/all_to_all | solution.py:456
  63.6 0.7 multiply_cosine_fusion.cosine_ref
  64.2 0.1 reshape.219
  64.3 0.8 copy.32.limit_ref
  65.1 0.6 convert_element_type.63.own_ref
  65.7 0.1 reduce_max.9
  65.8 0.2 select_reduce_fusion
  66.0 0.5 negate_maximum_fusion.blocks_ref
  66.6 0.7 multiply_add_fusion.start_ref
  67.3 1.4 %fusion.12 = (f32[25,32,16]{2,1,0:T(8,128)}, f32[25,32,16]{2,1,0:T(8,128)}) fusion(f32[32]{0:T(128)S(1)} %minimum_convert_fusion, f32[32]{0:T(128)S(1)} %fusion.29, f32[25,16]{1,0:T(8,128)S(1)} %add_add_fusion.1), kind=kLoop, calls=%fused_computation.24 | loop fusion | flops 192000 | bytes 104256 | tf_op jit(solution)/shard_map/sqrt | solution.py:232
  68.6 15.0 %legendre_table.1 = (bf16[2,4,1600,512]{3,2,1,0:T(8,128)(2,1)}, bf16[2,4,1600,512]{3,2,1,0:T(8,128)(2,1)}) custom-call(s32[4]{0:T(128)} %negate_maximum_fusion.blocks_ref, f32[25,32,16]{2,1,0:T(8,128)} %get-tuple-element.24.growth_ref, f32[25,32,16]{2,1,0:T(8,128)} %get-tuple-element.23.damping_ref, f32[1,512]{1,0:T(1,128)} %multiply_cosine_fusion.cosine_ref, ...), custom_call_target="tpu_custom_call" | custom-call | flops 65536000 | bytes 26214400 | tf_op jit(solution)/shard_map/legendre_table/pallas_call | solution.py:289
  83.7 0.7 all-to-all-done.1
  84.3 0.1 reshape.222
  84.4 0.3 copy.30
  84.8 0.5 reshape.223
  85.3 0.1 broadcast_multiply_fusion
  85.3 0.2 slice.25
  85.5 1.3 %reverse = f32[200,512]{1,0:T(8,128)S(1)} reverse(f32[200,512]{1,0:T(8,128)S(1)} %bitcast.13), dimensions={1} | reverse | bytes 819200
  86.8 0.2 add_bitcast_fusion
  87.0 1.1 select_maximum_fusion.folded_ref
  88.1 19.7 %legendre_contract.1 = f32[4,50,400]{2,1,0:T(8,128)} custom-call(s32[4]{0:T(128)} %negate_maximum_fusion.blocks_ref, bf16[2,4,1600,512]{3,2,1,0:T(8,128)(2,1)} %get-tuple-element.9.high_ref, bf16[2,4,1600,512]{3,2,1,0:T(8,128)(2,1)} %get-tuple-element.10.low_ref, f32[2,256,512]{2,1,0:T(8,128)} %select_maximum_fusion.folded_ref, ...), custom_call_target="tpu_custom_call" | custom-call | flops 10066329600 | bytes 26214400 | tf_op jit(solution)/shard_map/legendre_contract/pallas_call | solution.py:378
  107.8 12.9 %all_to_all.15 = f32[4,50,400]{2,1,0:T(8,128)S(1)} all-to-all(f32[4,50,400]{2,1,0:T(8,128)} %legendre_contract.1), channel_id=1, replica_groups=mesh['member'=2,'lat'=4,'lev'=2,'fld'=2] {'lev','fld'}, dimensions={0} | all-to-all | bytes 640000 | tf_op jit(solution)/shard_map/all_to_all | solution.py:478
  120.7 1.0 reshape_transpose_reshape.3
  (17 shorter events, 0.3 us)
Async XLA Ops:
  0.8 16.4 %collective-permute-start.3 = (bf16[4,1,400]{2,1,0:T(2,128)(2,1)S(1)}, bf16[4,1,400]{2,1,0:T(2,128)(2,1)S(1)}, u32[]{:S(2)}, u32[]{:S(2)}) collective-permute-start(bf16[4,1,400]{2,1,0:T(2,128)(2,1)S(1)} %get-tuple-element.17), channel_id=1, source_target_pairs={{4,0},{8,4},{12,8},{0,12},{5,1},{9,5},{13,9},{1,13},{6,2},{10,6},{... | collective-permute-start | bytes 9608 | tf_op jit(solution)/shard_map/ppermute | solution.py:32
  5.9 11.8 %collective-permute-start.2 = (bf16[4,1,400]{2,1,0:T(2,128)(2,1)S(1)}, bf16[4,1,400]{2,1,0:T(2,128)(2,1)S(1)}, u32[]{:S(2)}, u32[]{:S(2)}) collective-permute-start(bf16[4,1,400]{2,1,0:T(2,128)(2,1)S(1)} %get-tuple-element.18), channel_id=1, source_target_pairs={{0,4},{4,8},{8,12},{12,0},{1,5},{5,9},{9,13},{13,1},{2,6},{6,10},{... | collective-permute-start | bytes 9608 | tf_op jit(solution)/shard_map/ppermute | solution.py:29
  7.1 11.3 %collective-permute-start = (bf16[4,200,1]{2,1,0:T(8,128)(2,1)S(1)}, bf16[4,200,1]{2,1,0:T(8,128)(2,1)S(1)}, u32[]{:S(2)}, u32[]{:S(2)}) collective-permute-start(bf16[4,200,1]{2,1,0:T(8,128)(2,1)S(1)} %get-tuple-element.20), channel_id=1, source_target_pairs={{0,1},{1,2},{2,3},{3,0},{4,5},{5,6},{6,7},{7,4},{8,9},{9,10},{10,1... | collective-permute-start | bytes 4808 | tf_op jit(solution)/shard_map/ppermute | solution.py:29
  7.2 11.2 %collective-permute-start.1 = (bf16[4,200,1]{2,1,0:T(8,128)(2,1)S(1)}, bf16[4,200,1]{2,1,0:T(8,128)(2,1)S(1)}, u32[]{:S(2)}, u32[]{:S(2)}) collective-permute-start(bf16[4,200,1]{2,1,0:T(8,128)(2,1)S(1)} %get-tuple-element.19), channel_id=1, source_target_pairs={{1,0},{2,1},{3,2},{0,3},{5,4},{6,5},{7,6},{4,7},{9,8},{10,9},{11,1... | collective-permute-start | bytes 4808 | tf_op jit(solution)/shard_map/ppermute | solution.py:32
  18.4 0.7 copy-start.1
  19.1 0.7 copy-start.2
  24.3 24.3 %all-to-all-start = ((f32[4,200,400]{2,1,0:T(8,128)}), f32[4,200,400]{2,1,0:T(8,128)S(1)}, u32[]{:S(2)}, u32[]{:S(2)}) async-start(f32[4,200,400]{2,1,0:T(8,128)} %advect.1), calls=%async_computation | async-start | bytes 3276800 | tf_op jit(solution)/shard_map/all_to_all | solution.py:453
  48.6 1.3 %copy-start = (f32[4,200,400]{2,1,0:T(8,128)}, f32[4,200,400]{2,1,0:T(8,128)S(1)}, u32[]{:S(2)}) copy-start(f32[4,200,400]{2,1,0:T(8,128)S(1)} %all-to-all-done) | copy-start | bytes 3840004
  58.3 26.0 %all-to-all-start.1 = ((f32[16,50,200]{2,1,0:T(8,128)}), f32[16,50,200]{2,1,0:T(8,128)S(1)}, u32[]{:S(2)}, u32[]{:S(2)}) async-start(f32[16,50,200]{2,1,0:T(8,128)} %fourier_transform.1), calls=%async_computation.1 | async-start | bytes 1835008 | tf_op jit(solution)/shard_map/all_to_all | solution.py:456

commit v5 on v4

--- a/solution.py
+++ b/solution.py
@@ -240,7 +240,7 @@
 
 
 def table_kernel(
-    blocks_ref, growth_ref, damping_ref, cosine_ref, start_ref, high_ref, low_ref
+    blocks_ref, growth_ref, damping_ref, cosine_ref, start_ref, table_ref
 ):
     shape = start_ref.shape
     cosine = jnp.broadcast_to(cosine_ref[...], shape)
@@ -252,20 +252,13 @@
         scale = jnp.exp(log_scale)
         growth = growth_ref[index]
         damping = damping_ref[index]
-        rows = []
         for offset in range(block_rows):
-            rows.append(current * scale)
+            first = pl.multiple_of(index * wide + offset // 2 * slots, slots)
+            table_ref[offset % 2, 0, pl.ds(first, slots)] = current * scale
             advanced = growth[:, offset : offset + 1] * (
                 cosine * current - damping[:, offset : offset + 1] * before
             )
             before, current = current, advanced
-            if offset % 4 == 3:
-                for parity in range(2):
-                    pair = jnp.concatenate([rows[offset - 3 + parity], rows[offset - 1 + parity]])
-                    high, low = split_high_low(pair)
-                    first = pl.multiple_of(index * wide + offset // 4 * 2 * slots, 2 * slots)
-                    high_ref[parity, 0, pl.ds(first, 2 * slots)] = high
-                    low_ref[parity, 0, pl.ds(first, 2 * slots)] = low
         biggest = jnp.maximum(jnp.abs(before), jnp.abs(current))
         return before / biggest, current / biggest, log_scale + jnp.log(biggest)
 
@@ -282,7 +275,7 @@
     lats = cosine.shape[1]
     rows = blocks * block_rows // 2 * slot_tile
     tiles = slots // slot_tile
-    out = jax.ShapeDtypeStruct((2, tiles, rows, lats), jnp.bfloat16)
+    out = jax.ShapeDtypeStruct((2, tiles, rows, lats), jnp.float32)
     coef_spec = pl.BlockSpec((blocks, slot_tile, block_rows), lambda i, used: (0, i, 0))
     out_spec = pl.BlockSpec((2, 1, rows, lats), lambda i, used: (0, i, 0, 0))
     size = 2 * tiles * rows * lats
@@ -297,9 +290,9 @@
                 pl.BlockSpec((1, lats), lambda i, used: (0, 0)),
                 pl.BlockSpec((slot_tile, lats), lambda i, used: (i, 0)),
             ],
-            out_specs=[out_spec, out_spec],
-        ),
-        out_shape=[out, out],
+            out_specs=out_spec,
+        ),
+        out_shape=out,
         cost_estimate=pl.CostEstimate(
             flops=10 * size, bytes_accessed=4 * size, transcendentals=size // 4
         ),
@@ -309,8 +302,7 @@
 
 def contract_kernel(
     blocks_ref,
-    high_ref,
-    low_ref,
+    table_ref,
     folded_ref,
     own_ref,
     limit_ref,
@@ -321,7 +313,7 @@
 ):
     tile = pl.program_id(0)
     step = pl.program_id(1)
-    rows = high_ref.shape[2]
+    rows = table_ref.shape[2]
     slots = own_ref.shape[0]
     orders = rows // slots
     _, lane_tiles, half, lanes = sums_ref.shape
@@ -339,7 +331,7 @@
         own = own_ref[...] > 0.0
         for parity in range(2):
             full = jnp.dot(
-                three_passes(high_ref[parity, 0], low_ref[parity, 0]),
+                three_passes(*split_high_low(table_ref[parity, 0])),
                 weight_ref[parity],
                 preferred_element_type=jnp.float32,
             )
@@ -363,9 +355,9 @@
 
 
 def contract_table(
-    blocks_used, high, low, folded, own, limit, levels, rows_own
+    blocks_used, table, folded, own, limit, levels, rows_own
 ):
-    _, tiles, rows, lats = high.shape
+    _, tiles, rows, lats = table.shape
     columns = folded.shape[1]
     block = order_tile // 2 * slot_tile
     order_total = 2 * rows // slot_tile
@@ -381,7 +373,6 @@
             num_scalar_prefetch=1,
             grid=(tiles, rows // block),
             in_specs=[
-                table_spec,
                 table_spec,
                 weight_spec,
                 pl.BlockSpec((slot_tile, columns), lambda i, j, used: (i, 0)),
@@ -401,7 +392,7 @@
             transcendentals=0,
         ),
         name="legendre_contract",
-    )(blocks_used, high, low, folded, own, limit)
+    )(blocks_used, table, folded, own, limit)
 
 
 def shards(tracer, wind_east, wind_north, keep_m, slot_wave):
@@ -434,7 +425,7 @@
     padded_waves = M - jnp.sum(jnp.where(placed, M - my_waves[None, :], 0), axis=1)
     longest = jnp.max((M - padded_waves).reshape(-1, slot_tile), axis=1)
     blocks_used = jnp.maximum(-(-longest // order_tile), 0)
-    table_high, table_low = legendre_table(
+    legendre = legendre_table(
         blocks_used, *legendre_setup(padded_waves, M, NLAT, half_lat, lat_padded)
     )
 
@@ -473,7 +464,7 @@
     own = jnp.any(column_of_row & placed[:, None, :], axis=2).astype(jnp.float32)
     limit = jnp.sum(jnp.where(column_of_row[0], M - my_waves[None, :], 0), axis=1)[:, None]
     result = contract_table(
-        blocks_used, table_high, table_low, folded, own, limit, levels, rows_own
+        blocks_used, legendre, folded, own, limit, levels, rows_own
     )
     result = lax.all_to_all(result, GROUP, split_axis=0, concat_axis=0, tiled=True)
     result = result.reshape(groups, own_levels, slots_own, 2, M).transpose(1, 0, 2, 3, 4)

time: 123 us -> 122 us (level)
  Pallas kernels: 56.1 us -> 53.3 us
  waiting for transfers between devices: 11.7 us -> 13.6 us
    all_to_all x1, waiting for transfers between devices: 0.69 us -> 2.57 us  [shards(): lax.all_to_all(fourier, ('lat',) + GROUP, split_axis=0, concat_axis=0, ti...]
    pallas_call x1, Pallas kernels: 15 us -> 13.1 us  [legendre_table(): pl.pallas_call(table_kernel, grid_spec=pltpu.PrefetchScalarGridSpec(num_s...]
  transfers between devices with their start and end apart: 6 -> 6, of which waited for: 2 -> 2; matrix products, arithmetic and copies ran while one was open for 14% -> 14% of each run, Pallas kernels for 19% -> 18%
where the time goes in v5:
time: 122 us; the launch traced here: 120 us
  Pallas kernels  53.3 us (44%)
  starting transfers between devices  15.7 us (13%)
  other arithmetic  14 us (11%)
  waiting for transfers between devices  13.6 us (11%)
  blocking collectives  12.6 us (10%)
  local copies, waits for them, and re-layouts  11.2 us (9%)
    pallas_call x1, Pallas kernels, contract_table(): pl.pallas_call(contract_kernel, grid_spec=pltpu.PrefetchScalarGridSpec(nu...  18.7 us
    pallas_call x1, Pallas kernels, legendre_table(): pl.pallas_call(table_kernel, grid_spec=pltpu.PrefetchScalarGridSpec(num_s...  13.1 us
    all_to_all x1, blocking collectives, shards(): lax.all_to_all(result, GROUP, split_axis=0, concat_axis=0, tiled=True)  12.6 us
    all_to_all x1, waiting for transfers between devices, shards(): lax.all_to_all(advected, GROUP, split_axis=0, concat_axis=0, tiled=True)  11 us
    pallas_call x1, Pallas kernels, fourier_transform(): pl.pallas_call(lambda *refs: fourier_kernel(rows_own, *refs), grid=(chunk...  8.47 us
    pallas_call x1, Pallas kernels, fourier_table(): pl.pallas_call(wave_table_kernel, grid=(rows // tall,), in_specs=[pl.Bloc...  8.34 us
    ppermute x2, starting transfers between devices, edges(): high = lax.ppermute(lax.slice_in_dim(block, 0, 1, axis=dim), axis, backward)  6.86 us
    all_to_all x1, starting transfers between devices, shards(): lax.all_to_all(fourier, ('lat',) + GROUP, split_axis=0, concat_axis=0, ti...  5.2 us
  transfers between devices with their start and end apart: 6, of which 2 were waited for; matrix products, arithmetic and copies ran while one was open for 14% of the time, Pallas kernels for 18%

profile of v5, /device:TPU:0, one launch (start us, length us, event | category | flops | bytes accessed | tf_op | source)
XLA Modules:
  0.0 120.5 jit_solution(10114975388632700659)
XLA Ops:
  0.0 0.8 fusion.30
  0.8 5.1 %collective-permute-start.3 = (bf16[4,1,400]{2,1,0:T(2,128)(2,1)S(1)}, bf16[4,1,400]{2,1,0:T(2,128)(2,1)S(1)}, u32[]{:S(2)}, u32[]{:S(2)}) collective-permute-start(bf16[4,1,400]{2,1,0:T(2,128)(2,1)S(1)} %get-tuple-element.13), channel_id=1, source_target_pairs={{4,0},{8,4},{12,8},{0,12},{5,1},{9,5},{13,9},{1,13},{6,2},{10,6},{... | collective-permute-start | bytes 9608 | tf_op jit(solution)/shard_map/ppermute | solution.py:32
  5.9 0.0 collective-permute-start.2
  5.9 1.2 fusion.31
  7.1 0.1 collective-permute-start
  7.2 1.7 %collective-permute-start.1 = (bf16[4,200,1]{2,1,0:T(8,128)(2,1)S(1)}, bf16[4,200,1]{2,1,0:T(8,128)(2,1)S(1)}, u32[]{:S(2)}, u32[]{:S(2)}) collective-permute-start(bf16[4,200,1]{2,1,0:T(8,128)(2,1)S(1)} %get-tuple-element.15), channel_id=1, source_target_pairs={{1,0},{2,1},{3,2},{0,3},{5,4},{6,5},{7,6},{4,7},{9,8},{10,9},{11,1... | collective-permute-start | bytes 4808 | tf_op jit(solution)/shard_map/ppermute | solution.py:32
  8.9 0.8 reshape_reshape.3
  9.7 0.1 copy.25
  9.8 0.1 copy.34
  9.9 0.1 mul.234
  10.0 0.1 broadcast_add_fusion
  10.1 0.1 add.214
  10.2 3.1 %fusion.7 = (f32[896,128]{1,0:T(8,128)}, f32[896,128]{1,0:T(8,128)}) fusion(s32[896]{0:T(1024)S(1)} %mul.234), kind=kLoop, calls=%fused_computation.17 | loop fusion | flops 1032192 | bytes 921088 | tf_op jit(solution)/shard_map/sin | solution.py:44
  13.2 0.1 fusion.19
  13.3 0.2 copy.27
  13.5 2.5 %sine_multiply_fusion = (f32[896,16]{1,0:T(8,128)}, f32[896,16]{1,0:T(8,128)}) fusion(f32[896,16]{1,0:T(8,128)S(1)} %copy.27), kind=kLoop, calls=%fused_computation.19 | loop fusion | flops 43008 | bytes 172032 | tf_op jit(solution)/shard_map/mul | solution.py:44
  16.0 0.8 broadcast_subtract_fusion
  16.8 0.2 convert_reduce_fusion
  17.0 0.1 select_reduce_fusion.2
  17.2 0.0 collective-permute-done.3
  17.2 0.6 convert_multiply_fusion.below_ref
  17.8 0.0 collective-permute-done.2
  17.8 0.6 convert_multiply_fusion.1.above_ref
  18.4 0.0 collective-permute-done.west_ref
  18.4 0.0 copy-start.1
  18.4 0.0 collective-permute-done.1.east_ref
  18.4 0.7 copy-done.1
  19.1 0.0 copy-start.2
  19.1 0.7 copy-done.2
  19.7 4.6 %advect.1 = f32[4,200,400]{2,1,0:T(8,128)} custom-call(bf16[4,200,400]{2,1,0:T(8,128)(2,1)} %tracer_ref.1, bf16[4,200,400]{2,1,0:T(8,128)(2,1)} %east_wind_ref.1, bf16[4,200,400]{2,1,0:T(8,128)(2,1)} %north_wind_ref.1, bf16[4,200,1]{2,1,0:T(8,128)(2,1)} %copy-done.1, bf16[4,200,1]{2,1,0:T(8,128)(2,1)} %copy-done.2, ...), custom_call_target="tpu_custom_call" | custom-call | flops 3200000 | bytes 3200000 | tf_op jit(solution)/shard_map/advect/pallas_call | solution.py:119
  24.4 3.6 %all-to-all-start = ((f32[4,200,400]{2,1,0:T(8,128)}), f32[4,200,400]{2,1,0:T(8,128)S(1)}, u32[]{:S(2)}, u32[]{:S(2)}) async-start(f32[4,200,400]{2,1,0:T(8,128)} %advect.1), calls=%async_computation | async-start | bytes 3276800 | tf_op jit(solution)/shard_map/all_to_all | solution.py:444
  28.0 1.0 broadcast_in_dim_reshape.3.refs_3_
  28.9 0.1 copy.31
  29.0 8.3 %fourier_table.1 = (bf16[4,896,512]{2,1,0:T(8,128)(2,1)}, bf16[4,896,512]{2,1,0:T(8,128)(2,1)}) custom-call(f32[896,16]{1,0:T(8,128)} %get-tuple-element.18.base_cos_ref, f32[896,16]{1,0:T(8,128)} %get-tuple-element.17.base_sin_ref, f32[896,128]{1,0:T(8,128)} %get-tuple-element.22.lane_cos_ref, f32[896,128]{1,0:T(8,128)} %get-tuple-element.21.lane_sin_ref), custom_call_target="tpu_custom_call" | custom-call | flops 14680064 | bytes 7340032 | tf_op jit(solution)/shard_map/fourier_table/pallas_call | solution.py:75
  37.3 0.1 select_reduce_fusion.1
  37.5 0.2 and_reduce_fusion
  37.7 11.0 %all-to-all-done = f32[4,200,400]{2,1,0:T(8,128)S(1)} async-done(((f32[4,200,400]{2,1,0:T(8,128)}), f32[4,200,400]{2,1,0:T(8,128)S(1)}, u32[]{:S(2)}, u32[]{:S(2)}) %all-to-all-start) | async-done | bytes 1280032 | tf_op jit(solution)/shard_map/all_to_all | solution.py:444
  48.6 0.0 copy-start
  48.7 1.3 %copy-done = f32[4,200,400]{2,1,0:T(8,128)} copy-done((f32[4,200,400]{2,1,0:T(8,128)}, f32[4,200,400]{2,1,0:T(8,128)S(1)}, u32[]{:S(2)}) %copy-start) | copy-done | bytes 1280024
  49.9 8.5 %fourier_transform.1 = f32[16,50,200]{2,1,0:T(8,128)} custom-call(bf16[4,896,512]{2,1,0:T(8,128)(2,1)} %get-tuple-element.7.refs_0_, bf16[4,896,512]{2,1,0:T(8,128)(2,1)} %get-tuple-element.8.refs_1_, f32[4,1,200,400]{3,2,1,0:T(8,128)} %bitcast.11, s32[896,1]{1,0:T(8,128)} %broadcast_in_dim_reshape.3.refs_3_, s32[1,200]{1,0:T(1,128)} %bitcast.15), custom_call_target="tpu_custom_call" | custom-call | flops 1720320000 | bytes 5734400 | tf_op jit(solution)/shard_map/fourier_transform/pallas_call | solution.py:190
  58.4 5.2 %all-to-all-start.1 = ((f32[16,50,200]{2,1,0:T(8,128)}), f32[16,50,200]{2,1,0:T(8,128)S(1)}, u32[]{:S(2)}, u32[]{:S(2)}) async-start(f32[16,50,200]{2,1,0:T(8,128)} %fourier_transform.1), calls=%async_computation.1 | async-start | bytes 1835008 | tf_op jit(solution)/shard_map/all_to_all | solution.py:447
  63.6 0.6 multiply_cosine_fusion.cosine_ref
  64.2 0.1 reshape.219
  64.3 0.8 copy.32.limit_ref
  65.1 0.6 convert_element_type.63.own_ref
  65.7 0.1 reduce_max.9
  65.8 0.2 select_reduce_fusion
  66.0 0.6 negate_maximum_fusion.blocks_ref
  66.6 0.7 multiply_add_fusion.start_ref
  67.3 1.4 %fusion.12 = (f32[25,32,16]{2,1,0:T(8,128)}, f32[25,32,16]{2,1,0:T(8,128)}) fusion(f32[32]{0:T(128)S(1)} %minimum_convert_fusion, f32[32]{0:T(128)S(1)} %fusion.29, f32[25,16]{1,0:T(8,128)S(1)} %add_add_fusion.1), kind=kLoop, calls=%fused_computation.24 | loop fusion | flops 192000 | bytes 104256 | tf_op jit(solution)/shard_map/sqrt | solution.py:232
  68.7 13.1 %legendre_table.1.table_ref = f32[2,4,1600,512]{3,2,1,0:T(8,128)} custom-call(s32[4]{0:T(128)} %negate_maximum_fusion.blocks_ref, f32[25,32,16]{2,1,0:T(8,128)} %get-tuple-element.20.growth_ref, f32[25,32,16]{2,1,0:T(8,128)} %get-tuple-element.19.damping_ref, f32[1,512]{1,0:T(1,128)} %multiply_cosine_fusion.cosine_ref, f32[32,512]{1,0:T(8,128)} %multiply_add_fusion.start_ref), custom_call_target="tpu_custom_call" | custom-call | flops 65536000 | bytes 26214400 | tf_op jit(solution)/shard_map/legendre_table/pallas_call | solution.py:282
  81.8 2.6 %all-to-all-done.1 = f32[16,50,200]{2,1,0:T(8,128)S(1)} async-done(((f32[16,50,200]{2,1,0:T(8,128)}), f32[16,50,200]{2,1,0:T(8,128)S(1)}, u32[]{:S(2)}, u32[]{:S(2)}) %all-to-all-start.1) | async-done | bytes 640032 | tf_op jit(solution)/shard_map/all_to_all | solution.py:447
  84.4 0.1 reshape.222
  84.5 0.3 copy.30
  84.8 0.5 reshape.223
  85.3 0.1 broadcast_multiply_fusion
  85.4 0.2 slice.25
  85.5 1.3 %reverse = f32[200,512]{1,0:T(8,128)S(1)} reverse(f32[200,512]{1,0:T(8,128)S(1)} %bitcast.13), dimensions={1} | reverse | bytes 819200
  86.8 0.2 add_bitcast_fusion
  87.1 1.1 select_maximum_fusion.folded_ref
  88.2 18.7 %legendre_contract.1 = f32[4,50,400]{2,1,0:T(8,128)} custom-call(s32[4]{0:T(128)} %negate_maximum_fusion.blocks_ref, f32[2,4,1600,512]{3,2,1,0:T(8,128)} %legendre_table.1.table_ref, f32[2,256,512]{2,1,0:T(8,128)} %select_maximum_fusion.folded_ref, f32[32,256]{1,0:T(8,128)} %convert_element_type.63.own_ref, s32[256,1]{1,0:T(8,128)} %copy.32.limit_ref), custom_call_target="tpu_custom_call" | custom-call | flops 10066329600 | bytes 26214400 | tf_op jit(solution)/shard_map/legendre_contract/pallas_call | solution.py:370
  106.9 12.6 %all_to_all.15 = f32[4,50,400]{2,1,0:T(8,128)S(1)} all-to-all(f32[4,50,400]{2,1,0:T(8,128)} %legendre_contract.1), channel_id=1, replica_groups=mesh['member'=2,'lat'=4,'lev'=2,'fld'=2] {'lev','fld'}, dimensions={0} | all-to-all | bytes 640000 | tf_op jit(solution)/shard_map/all_to_all | solution.py:469
  119.5 1.0 reshape_transpose_reshape.3
  (17 shorter events, 0.3 us)
Async XLA Ops:
  0.8 16.4 %collective-permute-start.3 = (bf16[4,1,400]{2,1,0:T(2,128)(2,1)S(1)}, bf16[4,1,400]{2,1,0:T(2,128)(2,1)S(1)}, u32[]{:S(2)}, u32[]{:S(2)}) collective-permute-start(bf16[4,1,400]{2,1,0:T(2,128)(2,1)S(1)} %get-tuple-element.13), channel_id=1, source_target_pairs={{4,0},{8,4},{12,8},{0,12},{5,1},{9,5},{13,9},{1,13},{6,2},{10,6},{... | collective-permute-start | bytes 9608 | tf_op jit(solution)/shard_map/ppermute | solution.py:32
  5.9 11.9 %collective-permute-start.2 = (bf16[4,1,400]{2,1,0:T(2,128)(2,1)S(1)}, bf16[4,1,400]{2,1,0:T(2,128)(2,1)S(1)}, u32[]{:S(2)}, u32[]{:S(2)}) collective-permute-start(bf16[4,1,400]{2,1,0:T(2,128)(2,1)S(1)} %get-tuple-element.14), channel_id=1, source_target_pairs={{0,4},{4,8},{8,12},{12,0},{1,5},{5,9},{9,13},{13,1},{2,6},{6,10},{... | collective-permute-start | bytes 9608 | tf_op jit(solution)/shard_map/ppermute | solution.py:29
  7.1 11.3 %collective-permute-start = (bf16[4,200,1]{2,1,0:T(8,128)(2,1)S(1)}, bf16[4,200,1]{2,1,0:T(8,128)(2,1)S(1)}, u32[]{:S(2)}, u32[]{:S(2)}) collective-permute-start(bf16[4,200,1]{2,1,0:T(8,128)(2,1)S(1)} %get-tuple-element.16), channel_id=1, source_target_pairs={{0,1},{1,2},{2,3},{3,0},{4,5},{5,6},{6,7},{7,4},{8,9},{9,10},{10,1... | collective-permute-start | bytes 4808 | tf_op jit(solution)/shard_map/ppermute | solution.py:29
  7.2 11.2 %collective-permute-start.1 = (bf16[4,200,1]{2,1,0:T(8,128)(2,1)S(1)}, bf16[4,200,1]{2,1,0:T(8,128)(2,1)S(1)}, u32[]{:S(2)}, u32[]{:S(2)}) collective-permute-start(bf16[4,200,1]{2,1,0:T(8,128)(2,1)S(1)} %get-tuple-element.15), channel_id=1, source_target_pairs={{1,0},{2,1},{3,2},{0,3},{5,4},{6,5},{7,6},{4,7},{9,8},{10,9},{11,1... | collective-permute-start | bytes 4808 | tf_op jit(solution)/shard_map/ppermute | solution.py:32
  18.4 0.7 copy-start.1
  19.1 0.7 copy-start.2
  24.4 24.3 %all-to-all-start = ((f32[4,200,400]{2,1,0:T(8,128)}), f32[4,200,400]{2,1,0:T(8,128)S(1)}, u32[]{:S(2)}, u32[]{:S(2)}) async-start(f32[4,200,400]{2,1,0:T(8,128)} %advect.1), calls=%async_computation | async-start | bytes 3276800 | tf_op jit(solution)/shard_map/all_to_all | solution.py:444
  48.6 1.3 %copy-start = (f32[4,200,400]{2,1,0:T(8,128)}, f32[4,200,400]{2,1,0:T(8,128)S(1)}, u32[]{:S(2)}) copy-start(f32[4,200,400]{2,1,0:T(8,128)S(1)} %all-to-all-done) | copy-start | bytes 3840004
  58.4 26.0 %all-to-all-start.1 = ((f32[16,50,200]{2,1,0:T(8,128)}), f32[16,50,200]{2,1,0:T(8,128)S(1)}, u32[]{:S(2)}, u32[]{:S(2)}) async-start(f32[16,50,200]{2,1,0:T(8,128)} %fourier_transform.1), calls=%async_computation.1 | async-start | bytes 1835008 | tf_op jit(solution)/shard_map/all_to_all | solution.py:447
